TPU v7x, 256 devices: a whole 4x4x8 slice. The times are simulated.
256 devices in a mesh: blk: 32 (over y_hi, z, core), lag: 8 (over y_lo, x).
Axes of the slice: x: 4, y: 4 (y_hi: 2, y_lo: 2; y = y_hi * 2 + y_lo), z: 8, core: 2. Of those that a mesh axis runs over, the one named last changes fastest.
Arguments:
- spectra: bfloat16 [4096, 3, 2, 1024], P('blk', None, None, 'lag'), may hold values from -6 to 6
- band: int32 [4096, 2], P('blk'), may hold values from 0 to 1024, as said below
- pair_lists: int32 [32, 17, 96, 2], P('blk'), may hold values from 0 to 127
- pair_counts: int32 [32, 17], P('blk'), may hold values from 32 to 96, as said below
Outputs:
- gradient: float32 [4096, 3, 2, 1024], P('blk', None, None, 'lag')
Inputs may be any that keep to these rules, and one draw needn't show every extreme that they name: band[s, 0] < band[s, 1]; band[s, 0] is at most 128 and band[s, 1] at least 896; some station starts at 0 and some ends at 1024. `pair_counts`: at least a third of the slots are used; in every block one offset uses all 96 slots.
All inputs are finite; a program needn't handle non-finite values.
Results may differ from a plain program's by a relative error of at most 0.0045.
Values may be sent and summed in bfloat16 or wider, within the bound.
No kernel may reach another device: no remote copies, remote signals or barrier semaphores. Data moves between devices by JAX's collectives and lax.ppermute only.
A program may use at most 64 MiB of HBM per device.

v0:
```python
import math

import jax
import jax.numpy as jnp
from jax import lax
from jax.sharding import PartitionSpec as P


def from_behind(block, axis, distance):
    devices = range(lax.axis_size(axis))
    route = [((i - distance) % len(devices), i) for i in devices]
    return lax.ppermute(block, axis, route)


def phase_table(freq_ids, lag_ids, lag_total, freq_total):
    turns = freq_ids[:, None] * lag_ids[None, :] % lag_total
    angle = turns.astype(jnp.float32) * (2.0 * jnp.pi / lag_total)
    factor = 1.0 / jnp.sqrt(jnp.float32(freq_total))
    return jnp.stack([jnp.cos(angle) * factor, -jnp.sin(angle) * factor], 0).astype(jnp.bfloat16)


def whiten(spectra, band, freq_ids):
    values = spectra.astype(jnp.float32)
    meansq = jnp.mean(values * values, axis=(1, 2))
    inside = (freq_ids[None, :] >= band[:, 0:1]) & (freq_ids[None, :] < band[:, 1:2])
    factor = jnp.where(inside, 1.0 / jnp.sqrt(jnp.maximum(meansq, 0.25)), 0.0)
    return (values * factor[:, None, None, :]).astype(jnp.bfloat16)


def on_device(spectra, band, pair_lists, pair_counts):
    stations, comps, parts, bins_local = spectra.shape
    slots = pair_lists.shape[2]
    steps = pair_lists.shape[1]
    lanes = lax.axis_size("lag")
    freq_total = bins_local * lanes
    lag_total = 2 * freq_total
    lag_local = lag_total // lanes
    width = comps * parts * bins_local
    lane = lax.axis_index("lag")
    freq_ids = lane * bins_local + jnp.arange(bins_local, dtype=jnp.int32)
    lag_ids = lane * lag_local + jnp.arange(lag_local, dtype=jnp.int32)
    resident = whiten(spectra, band, freq_ids)
    local_table = phase_table(
        freq_ids, jnp.arange(lag_total, dtype=jnp.int32), lag_total, freq_total
    )
    weight = 1.0 + 3.0 * lag_ids.astype(jnp.float32) / lag_total
    station_ids = jnp.arange(stations, dtype=jnp.int32)
    slot_ids = jnp.arange(slots, dtype=jnp.int32)

    def forward(cross):
        return lax.psum_scatter(
            jnp.einsum("prf,rft->tp", cross, local_table, preferred_element_type=jnp.float32),
            "lag",
            scatter_dimension=0,
            tiled=True,
        ).T

    def back(piece):
        return jnp.einsum("pt,rft->prf", piece, local_table, preferred_element_type=jnp.float32)

    def correlate(arriving, pairs, count):
        first = pairs[:, 0]
        second = pairs[:, 1]
        pick_first = (first[:, None] == station_ids[None, :]).astype(jnp.bfloat16)
        pick_second = (second[:, None] == station_ids[None, :]).astype(jnp.bfloat16)
        rows_a = jnp.dot(
            pick_first, resident.reshape(stations, width), preferred_element_type=jnp.float32
        )
        rows_b = jnp.dot(
            pick_second, arriving.reshape(stations, width), preferred_element_type=jnp.float32
        )
        rows_a = rows_a.reshape(slots, comps, parts, bins_local)
        rows_b = rows_b.reshape(slots, comps, parts, bins_local)
        real_a, imag_a = (rows_a[:, :, 0], rows_a[:, :, 1])
        real_b, imag_b = (rows_b[:, :, 0], rows_b[:, :, 1])
        valid = (slot_ids < count).astype(jnp.float32)[:, None]
        cross_real = jnp.sum(real_a * real_b + imag_a * imag_b, axis=1) * valid
        cross_imag = jnp.sum(imag_a * real_b - real_a * imag_b, axis=1) * valid
        cross = jnp.stack([cross_real, cross_imag], 1).astype(jnp.bfloat16)
        lagged = forward(cross)
        energy = lax.psum(jnp.sum(weight[None, :] * lagged * lagged, axis=1) / lag_total, "lag")
        adjoint = (weight[None, :] * lagged / jnp.sqrt(energy + 1e-05)[:, None]).astype(
            jnp.bfloat16
        )
        spectral = back(lax.all_gather(adjoint, "lag", axis=1, tiled=True))
        adj_real = spectral[:, None, 0]
        adj_imag = spectral[:, None, 1]
        near = jnp.stack(
            [adj_real * real_b - adj_imag * imag_b, adj_real * imag_b + adj_imag * real_b], 2
        )
        far = jnp.stack(
            [adj_real * real_a + adj_imag * imag_a, adj_real * imag_a - adj_imag * real_a], 2
        )
        near = near.astype(jnp.bfloat16).reshape(slots, width)
        far = far.astype(jnp.bfloat16).reshape(slots, width)
        own = jnp.einsum("ps,pw->sw", pick_first, near, preferred_element_type=jnp.float32)
        return (own, far, second, pick_second)

    def visit(step, arriving, total, carried):
        own, far, second, pick_second = correlate(
            arriving, pair_lists[0, step], pair_counts[0, step]
        )
        total = total + own
        carried = carried + jnp.einsum(
            "ps,pw->sw", pick_second, far, preferred_element_type=jnp.float32
        )
        return (total, carried)

    def advance(step, state):
        arriving, total, carried = state
        arriving = from_behind(arriving, "blk", 1)
        carried = from_behind(carried, "blk", 1)
        total, carried = visit(step, arriving, total, carried)
        return (arriving, total, carried)

    start_carried = jnp.zeros((stations, width), jnp.float32)
    total, carried = visit(0, resident, jnp.zeros((stations, width), jnp.float32), start_carried)
    arriving, total, carried = lax.fori_loop(1, steps, advance, (resident, total, carried))
    total = total + from_behind(carried, "blk", -(steps - 1))
    gradient = total / math.sqrt(slots)
    return gradient.reshape(stations, comps, parts, bins_local)


def solution(mesh):
    in_specs = (
        P("blk", None, None, "lag"),
        P("blk", None),
        P("blk", None, None, None),
        P("blk", None),
    )
    out_specs = P("blk", None, None, "lag")
    return jax.shard_map(
        on_device, mesh=mesh, in_specs=in_specs, out_specs=out_specs, check_vma=False
    )
```

profile of v0, /device:TPU:1, one launch (start us, length us, event | category | flops | bytes accessed | tf_op | source)
XLA Modules:
  0.0 1670.2 jit_solution(6176703667037175156)
XLA Ops:
  16.2 39.6 %reduce-scatter.3.cloned.1.call-done = f32[256,96]{0,1:T(8,128)} async-done(((f32[2048,96]{0,1:T(8,128)}), f32[256,96]{0,1:T(8,128)}) %reduce-scatter.3.cloned.1.call-update) | async-done | bytes 98320 | tf_op jit(solution)/shard_map/reduce_scatter | solution.py:51
  71.8 22.4 %all_gather.13 = bf16[96,2048]{1,0:T(8,128)(2,1)S(1)} all-gather(bf16[96,256]{1,0:T(8,128)(2,1)S(1)} %fusion.43), channel_id=1, replica_groups=mesh['blk'=32,'lag'=8] {'lag'}, dimensions={1}, use_global_device_ids=true | all-gather | bytes 442368 | tf_op jit(solution)/shard_map/all_gather | solution.py:85
  95.9 1558.3 %while.21 = (s32[]{:T(128)}, bf16[128,3,2,128]{0,3,2,1:T(8,128)(2,1)S(1)}, f32[128,768]{1,0:T(8,128)S(1)}, f32[128,768]{1,0:T(8,128)S(1)}, s32[1,17,96,2]{2,3,1,...) while((s32[]{:T(128)}, ...), condition=%wide.region_12.13_spmd.clone.clone, body=%wide.region_6.12_spmd.clone.clone.sunk | while | flops 278300032 | bytes 16166447 | solution.py:118
  96.0 16.1 collective-permute-start
  118.8 34.3 %reduce-scatter.5.cloned.1.call-done = f32[256,96]{0,1:T(8,128)} async-done(((f32[2048,96]{0,1:T(8,128)}), f32[256,96]{0,1:T(8,128)}) %reduce-scatter.5.cloned.1.call-update) | async-done | bytes 98320 | tf_op jit(solution)/shard_map/while/body/eval_jaxpr/reduce_scatter | solution.py:51
  169.2 22.4 %all_gather.17 = bf16[96,2048]{1,0:T(8,128)(2,1)S(1)} all-gather(bf16[96,256]{1,0:T(8,128)(2,1)S(1)} %fusion.96), channel_id=1, replica_groups=mesh['blk'=32,'lag'=8] {'lag'}, dimensions={1}, use_global_device_ids=true | all-gather | bytes 442368 | tf_op jit(solution)/shard_map/while/body/eval_jaxpr/all_gather | solution.py:85
  193.4 16.1 collective-permute-start
  216.2 34.3 %reduce-scatter.5.cloned.1.call-done = f32[256,96]{0,1:T(8,128)} async-done(((f32[2048,96]{0,1:T(8,128)}), f32[256,96]{0,1:T(8,128)}) %reduce-scatter.5.cloned.1.call-update) | async-done | bytes 98320 | tf_op jit(solution)/shard_map/while/body/eval_jaxpr/reduce_scatter | solution.py:51
  266.6 22.4 %all_gather.17 = bf16[96,2048]{1,0:T(8,128)(2,1)S(1)} all-gather(bf16[96,256]{1,0:T(8,128)(2,1)S(1)} %fusion.96), channel_id=1, replica_groups=mesh['blk'=32,'lag'=8] {'lag'}, dimensions={1}, use_global_device_ids=true | all-gather | bytes 442368 | tf_op jit(solution)/shard_map/while/body/eval_jaxpr/all_gather | solution.py:85
  290.8 16.0 collective-permute-start
  313.6 34.4 %reduce-scatter.5.cloned.1.call-done = f32[256,96]{0,1:T(8,128)} async-done(((f32[2048,96]{0,1:T(8,128)}), f32[256,96]{0,1:T(8,128)}) %reduce-scatter.5.cloned.1.call-update) | async-done | bytes 98320 | tf_op jit(solution)/shard_map/while/body/eval_jaxpr/reduce_scatter | solution.py:51
  364.0 22.6 %all_gather.17 = bf16[96,2048]{1,0:T(8,128)(2,1)S(1)} all-gather(bf16[96,256]{1,0:T(8,128)(2,1)S(1)} %fusion.96), channel_id=1, replica_groups=mesh['blk'=32,'lag'=8] {'lag'}, dimensions={1}, use_global_device_ids=true | all-gather | bytes 442368 | tf_op jit(solution)/shard_map/while/body/eval_jaxpr/all_gather | solution.py:85
  411.0 34.4 %reduce-scatter.5.cloned.1.call-done = f32[256,96]{0,1:T(8,128)} async-done(((f32[2048,96]{0,1:T(8,128)}), f32[256,96]{0,1:T(8,128)}) %reduce-scatter.5.cloned.1.call-update) | async-done | bytes 98320 | tf_op jit(solution)/shard_map/while/body/eval_jaxpr/reduce_scatter | solution.py:51
  461.6 22.3 %all_gather.17 = bf16[96,2048]{1,0:T(8,128)(2,1)S(1)} all-gather(bf16[96,256]{1,0:T(8,128)(2,1)S(1)} %fusion.96), channel_id=1, replica_groups=mesh['blk'=32,'lag'=8] {'lag'}, dimensions={1}, use_global_device_ids=true | all-gather | bytes 442368 | tf_op jit(solution)/shard_map/while/body/eval_jaxpr/all_gather | solution.py:85
  508.4 34.4 %reduce-scatter.5.cloned.1.call-done = f32[256,96]{0,1:T(8,128)} async-done(((f32[2048,96]{0,1:T(8,128)}), f32[256,96]{0,1:T(8,128)}) %reduce-scatter.5.cloned.1.call-update) | async-done | bytes 98320 | tf_op jit(solution)/shard_map/while/body/eval_jaxpr/reduce_scatter | solution.py:51
  558.2 22.7 %all_gather.17 = bf16[96,2048]{1,0:T(8,128)(2,1)S(1)} all-gather(bf16[96,256]{1,0:T(8,128)(2,1)S(1)} %fusion.96), channel_id=1, replica_groups=mesh['blk'=32,'lag'=8] {'lag'}, dimensions={1}, use_global_device_ids=true | all-gather | bytes 442368 | tf_op jit(solution)/shard_map/while/body/eval_jaxpr/all_gather | solution.py:85
  582.8 16.2 collective-permute-start
  605.8 34.4 %reduce-scatter.5.cloned.1.call-done = f32[256,96]{0,1:T(8,128)} async-done(((f32[2048,96]{0,1:T(8,128)}), f32[256,96]{0,1:T(8,128)}) %reduce-scatter.5.cloned.1.call-update) | async-done | bytes 98320 | tf_op jit(solution)/shard_map/while/body/eval_jaxpr/reduce_scatter | solution.py:51
  655.7 22.7 %all_gather.17 = bf16[96,2048]{1,0:T(8,128)(2,1)S(1)} all-gather(bf16[96,256]{1,0:T(8,128)(2,1)S(1)} %fusion.96), channel_id=1, replica_groups=mesh['blk'=32,'lag'=8] {'lag'}, dimensions={1}, use_global_device_ids=true | all-gather | bytes 442368 | tf_op jit(solution)/shard_map/while/body/eval_jaxpr/all_gather | solution.py:85
  680.2 16.2 collective-permute-start
  703.2 34.4 %reduce-scatter.5.cloned.1.call-done = f32[256,96]{0,1:T(8,128)} async-done(((f32[2048,96]{0,1:T(8,128)}), f32[256,96]{0,1:T(8,128)}) %reduce-scatter.5.cloned.1.call-update) | async-done | bytes 98320 | tf_op jit(solution)/shard_map/while/body/eval_jaxpr/reduce_scatter | solution.py:51
  753.1 22.8 %all_gather.17 = bf16[96,2048]{1,0:T(8,128)(2,1)S(1)} all-gather(bf16[96,256]{1,0:T(8,128)(2,1)S(1)} %fusion.96), channel_id=1, replica_groups=mesh['blk'=32,'lag'=8] {'lag'}, dimensions={1}, use_global_device_ids=true | all-gather | bytes 442368 | tf_op jit(solution)/shard_map/while/body/eval_jaxpr/all_gather | solution.py:85
  777.7 16.1 collective-permute-start
  800.6 34.4 %reduce-scatter.5.cloned.1.call-done = f32[256,96]{0,1:T(8,128)} async-done(((f32[2048,96]{0,1:T(8,128)}), f32[256,96]{0,1:T(8,128)}) %reduce-scatter.5.cloned.1.call-update) | async-done | bytes 98320 | tf_op jit(solution)/shard_map/while/body/eval_jaxpr/reduce_scatter | solution.py:51
  850.5 22.7 %all_gather.17 = bf16[96,2048]{1,0:T(8,128)(2,1)S(1)} all-gather(bf16[96,256]{1,0:T(8,128)(2,1)S(1)} %fusion.96), channel_id=1, replica_groups=mesh['blk'=32,'lag'=8] {'lag'}, dimensions={1}, use_global_device_ids=true | all-gather | bytes 442368 | tf_op jit(solution)/shard_map/while/body/eval_jaxpr/all_gather | solution.py:85
  875.0 16.2 collective-permute-start
  898.0 34.4 %reduce-scatter.5.cloned.1.call-done = f32[256,96]{0,1:T(8,128)} async-done(((f32[2048,96]{0,1:T(8,128)}), f32[256,96]{0,1:T(8,128)}) %reduce-scatter.5.cloned.1.call-update) | async-done | bytes 98320 | tf_op jit(solution)/shard_map/while/body/eval_jaxpr/reduce_scatter | solution.py:51
  948.5 22.4 %all_gather.17 = bf16[96,2048]{1,0:T(8,128)(2,1)S(1)} all-gather(bf16[96,256]{1,0:T(8,128)(2,1)S(1)} %fusion.96), channel_id=1, replica_groups=mesh['blk'=32,'lag'=8] {'lag'}, dimensions={1}, use_global_device_ids=true | all-gather | bytes 442368 | tf_op jit(solution)/shard_map/while/body/eval_jaxpr/all_gather | solution.py:85
  972.7 15.9 collective-permute-start
  995.4 34.4 %reduce-scatter.5.cloned.1.call-done = f32[256,96]{0,1:T(8,128)} async-done(((f32[2048,96]{0,1:T(8,128)}), f32[256,96]{0,1:T(8,128)}) %reduce-scatter.5.cloned.1.call-update) | async-done | bytes 98320 | tf_op jit(solution)/shard_map/while/body/eval_jaxpr/reduce_scatter | solution.py:51
  1045.8 22.4 %all_gather.17 = bf16[96,2048]{1,0:T(8,128)(2,1)S(1)} all-gather(bf16[96,256]{1,0:T(8,128)(2,1)S(1)} %fusion.96), channel_id=1, replica_groups=mesh['blk'=32,'lag'=8] {'lag'}, dimensions={1}, use_global_device_ids=true | all-gather | bytes 442368 | tf_op jit(solution)/shard_map/while/body/eval_jaxpr/all_gather | solution.py:85
  1070.1 16.0 collective-permute-start
  1092.9 34.3 %reduce-scatter.5.cloned.1.call-done = f32[256,96]{0,1:T(8,128)} async-done(((f32[2048,96]{0,1:T(8,128)}), f32[256,96]{0,1:T(8,128)}) %reduce-scatter.5.cloned.1.call-update) | async-done | bytes 98320 | tf_op jit(solution)/shard_map/while/body/eval_jaxpr/reduce_scatter | solution.py:51
  1143.2 22.4 %all_gather.17 = bf16[96,2048]{1,0:T(8,128)(2,1)S(1)} all-gather(bf16[96,256]{1,0:T(8,128)(2,1)S(1)} %fusion.96), channel_id=1, replica_groups=mesh['blk'=32,'lag'=8] {'lag'}, dimensions={1}, use_global_device_ids=true | all-gather | bytes 442368 | tf_op jit(solution)/shard_map/while/body/eval_jaxpr/all_gather | solution.py:85
  1167.4 15.9 collective-permute-start
  1190.2 34.5 %reduce-scatter.5.cloned.1.call-done = f32[256,96]{0,1:T(8,128)} async-done(((f32[2048,96]{0,1:T(8,128)}), f32[256,96]{0,1:T(8,128)}) %reduce-scatter.5.cloned.1.call-update) | async-done | bytes 98320 | tf_op jit(solution)/shard_map/while/body/eval_jaxpr/reduce_scatter | solution.py:51
  1240.1 22.7 %all_gather.17 = bf16[96,2048]{1,0:T(8,128)(2,1)S(1)} all-gather(bf16[96,256]{1,0:T(8,128)(2,1)S(1)} %fusion.96), channel_id=1, replica_groups=mesh['blk'=32,'lag'=8] {'lag'}, dimensions={1}, use_global_device_ids=true | all-gather | bytes 442368 | tf_op jit(solution)/shard_map/while/body/eval_jaxpr/all_gather | solution.py:85
  1264.6 16.2 collective-permute-start
  1287.6 34.4 %reduce-scatter.5.cloned.1.call-done = f32[256,96]{0,1:T(8,128)} async-done(((f32[2048,96]{0,1:T(8,128)}), f32[256,96]{0,1:T(8,128)}) %reduce-scatter.5.cloned.1.call-update) | async-done | bytes 98320 | tf_op jit(solution)/shard_map/while/body/eval_jaxpr/reduce_scatter | solution.py:51
  1338.1 22.5 %all_gather.17 = bf16[96,2048]{1,0:T(8,128)(2,1)S(1)} all-gather(bf16[96,256]{1,0:T(8,128)(2,1)S(1)} %fusion.96), channel_id=1, replica_groups=mesh['blk'=32,'lag'=8] {'lag'}, dimensions={1}, use_global_device_ids=true | all-gather | bytes 442368 | tf_op jit(solution)/shard_map/while/body/eval_jaxpr/all_gather | solution.py:85
  1385.0 34.4 %reduce-scatter.5.cloned.1.call-done = f32[256,96]{0,1:T(8,128)} async-done(((f32[2048,96]{0,1:T(8,128)}), f32[256,96]{0,1:T(8,128)}) %reduce-scatter.5.cloned.1.call-update) | async-done | bytes 98320 | tf_op jit(solution)/shard_map/while/body/eval_jaxpr/reduce_scatter | solution.py:51
  1434.9 22.7 %all_gather.17 = bf16[96,2048]{1,0:T(8,128)(2,1)S(1)} all-gather(bf16[96,256]{1,0:T(8,128)(2,1)S(1)} %fusion.96), channel_id=1, replica_groups=mesh['blk'=32,'lag'=8] {'lag'}, dimensions={1}, use_global_device_ids=true | all-gather | bytes 442368 | tf_op jit(solution)/shard_map/while/body/eval_jaxpr/all_gather | solution.py:85
  1459.4 16.2 collective-permute-start
  1482.4 34.4 %reduce-scatter.5.cloned.1.call-done = f32[256,96]{0,1:T(8,128)} async-done(((f32[2048,96]{0,1:T(8,128)}), f32[256,96]{0,1:T(8,128)}) %reduce-scatter.5.cloned.1.call-update) | async-done | bytes 98320 | tf_op jit(solution)/shard_map/while/body/eval_jaxpr/reduce_scatter | solution.py:51
  1533.0 22.3 %all_gather.17 = bf16[96,2048]{1,0:T(8,128)(2,1)S(1)} all-gather(bf16[96,256]{1,0:T(8,128)(2,1)S(1)} %fusion.96), channel_id=1, replica_groups=mesh['blk'=32,'lag'=8] {'lag'}, dimensions={1}, use_global_device_ids=true | all-gather | bytes 442368 | tf_op jit(solution)/shard_map/while/body/eval_jaxpr/all_gather | solution.py:85
  1557.1 16.0 collective-permute-start
  1579.8 34.4 %reduce-scatter.5.cloned.1.call-done = f32[256,96]{0,1:T(8,128)} async-done(((f32[2048,96]{0,1:T(8,128)}), f32[256,96]{0,1:T(8,128)}) %reduce-scatter.5.cloned.1.call-update) | async-done | bytes 98320 | tf_op jit(solution)/shard_map/while/body/eval_jaxpr/reduce_scatter | solution.py:51
  1629.7 22.7 %all_gather.17 = bf16[96,2048]{1,0:T(8,128)(2,1)S(1)} all-gather(bf16[96,256]{1,0:T(8,128)(2,1)S(1)} %fusion.96), channel_id=1, replica_groups=mesh['blk'=32,'lag'=8] {'lag'}, dimensions={1}, use_global_device_ids=true | all-gather | bytes 442368 | tf_op jit(solution)/shard_map/while/body/eval_jaxpr/all_gather | solution.py:85
  (540 shorter events, 472.4 us)
Async XLA Ops:
  6.5 49.2 %reduce-scatter.3.cloned.1.call-start = ((), (), s32[]{:S(2)}) async-start(), calls=%async_computation.2 | async-start | bytes 884736 | tf_op jit(solution)/shard_map/reduce_scatter | solution.py:51
  95.9 57.2 %reduce-scatter.5.cloned.1.call-start = ((), (), s32[]{:S(2)}) async-start(), calls=%async_computation.3 | async-start | bytes 884736 | tf_op jit(solution)/shard_map/while/body/eval_jaxpr/reduce_scatter | solution.py:51
  96.0 18.7 %collective-permute-start = (bf16[128,3,2,128]{0,3,2,1:T(8,128)(2,1)S(1)}, bf16[128,3,2,128]{0,3,2,1:T(8,128)(2,1)S(1)}, u32[]{:S(2)}, u32[]{:S(2)}) collective-permute-start(bf16[128,3,2,128]{0,3,2,1:T(8,128)(2,1)S(1)} %get-tuple-element.474), channel_id=1, source_target_pairs={{248,0},{0,8},{8,16},{16,24},{24,32},{32,40},{40,48},{48,56},{56,6... | collective-permute-start | bytes 589832 | tf_op jit(solution)/shard_map/while/body/eval_jaxpr/ppermute | solution.py:12
  116.2 76.7 %collective-permute-start.1 = (f32[128,768]{1,0:T(8,128)S(1)}, f32[128,768]{1,0:T(8,128)S(1)}, u32[]{:S(2)}, u32[]{:S(2)}) collective-permute-start(f32[128,768]{1,0:T(8,128)S(1)} %get-tuple-element.476), channel_id=1, source_target_pairs={{248,0},{0,8},{8,16},{16,24},{24,32},{32,40},{40,48},{48,56},{56,6... | collective-permute-start | bytes 1179656 | tf_op jit(solution)/shard_map/while/body/eval_jaxpr/ppermute | solution.py:12
  193.3 57.2 %reduce-scatter.5.cloned.1.call-start = ((), (), s32[]{:S(2)}) async-start(), calls=%async_computation.3 | async-start | bytes 884736 | tf_op jit(solution)/shard_map/while/body/eval_jaxpr/reduce_scatter | solution.py:51
  193.4 18.7 %collective-permute-start = (bf16[128,3,2,128]{0,3,2,1:T(8,128)(2,1)S(1)}, bf16[128,3,2,128]{0,3,2,1:T(8,128)(2,1)S(1)}, u32[]{:S(2)}, u32[]{:S(2)}) collective-permute-start(bf16[128,3,2,128]{0,3,2,1:T(8,128)(2,1)S(1)} %get-tuple-element.474), channel_id=1, source_target_pairs={{248,0},{0,8},{8,16},{16,24},{24,32},{32,40},{40,48},{48,56},{56,6... | collective-permute-start | bytes 589832 | tf_op jit(solution)/shard_map/while/body/eval_jaxpr/ppermute | solution.py:12
  213.6 76.7 %collective-permute-start.1 = (f32[128,768]{1,0:T(8,128)S(1)}, f32[128,768]{1,0:T(8,128)S(1)}, u32[]{:S(2)}, u32[]{:S(2)}) collective-permute-start(f32[128,768]{1,0:T(8,128)S(1)} %get-tuple-element.476), channel_id=1, source_target_pairs={{248,0},{0,8},{8,16},{16,24},{24,32},{32,40},{40,48},{48,56},{56,6... | collective-permute-start | bytes 1179656 | tf_op jit(solution)/shard_map/while/body/eval_jaxpr/ppermute | solution.py:12
  290.8 57.2 %reduce-scatter.5.cloned.1.call-start = ((), (), s32[]{:S(2)}) async-start(), calls=%async_computation.3 | async-start | bytes 884736 | tf_op jit(solution)/shard_map/while/body/eval_jaxpr/reduce_scatter | solution.py:51
  290.8 18.6 %collective-permute-start = (bf16[128,3,2,128]{0,3,2,1:T(8,128)(2,1)S(1)}, bf16[128,3,2,128]{0,3,2,1:T(8,128)(2,1)S(1)}, u32[]{:S(2)}, u32[]{:S(2)}) collective-permute-start(bf16[128,3,2,128]{0,3,2,1:T(8,128)(2,1)S(1)} %get-tuple-element.474), channel_id=1, source_target_pairs={{248,0},{0,8},{8,16},{16,24},{24,32},{32,40},{40,48},{48,56},{56,6... | collective-permute-start | bytes 589832 | tf_op jit(solution)/shard_map/while/body/eval_jaxpr/ppermute | solution.py:12
  311.0 76.9 %collective-permute-start.1 = (f32[128,768]{1,0:T(8,128)S(1)}, f32[128,768]{1,0:T(8,128)S(1)}, u32[]{:S(2)}, u32[]{:S(2)}) collective-permute-start(f32[128,768]{1,0:T(8,128)S(1)} %get-tuple-element.476), channel_id=1, source_target_pairs={{248,0},{0,8},{8,16},{16,24},{24,32},{32,40},{40,48},{48,56},{56,6... | collective-permute-start | bytes 1179656 | tf_op jit(solution)/shard_map/while/body/eval_jaxpr/ppermute | solution.py:12
  388.3 57.1 %reduce-scatter.5.cloned.1.call-start = ((), (), s32[]{:S(2)}) async-start(), calls=%async_computation.3 | async-start | bytes 884736 | tf_op jit(solution)/shard_map/while/body/eval_jaxpr/reduce_scatter | solution.py:51
  408.4 76.9 %collective-permute-start.1 = (f32[128,768]{1,0:T(8,128)S(1)}, f32[128,768]{1,0:T(8,128)S(1)}, u32[]{:S(2)}, u32[]{:S(2)}) collective-permute-start(f32[128,768]{1,0:T(8,128)S(1)} %get-tuple-element.476), channel_id=1, source_target_pairs={{248,0},{0,8},{8,16},{16,24},{24,32},{32,40},{40,48},{48,56},{56,6... | collective-permute-start | bytes 1179656 | tf_op jit(solution)/shard_map/while/body/eval_jaxpr/ppermute | solution.py:12
  485.6 57.2 %reduce-scatter.5.cloned.1.call-start = ((), (), s32[]{:S(2)}) async-start(), calls=%async_computation.3 | async-start | bytes 884736 | tf_op jit(solution)/shard_map/while/body/eval_jaxpr/reduce_scatter | solution.py:51
  485.7 18.5 %collective-permute-start = (bf16[128,3,2,128]{0,3,2,1:T(8,128)(2,1)S(1)}, bf16[128,3,2,128]{0,3,2,1:T(8,128)(2,1)S(1)}, u32[]{:S(2)}, u32[]{:S(2)}) collective-permute-start(bf16[128,3,2,128]{0,3,2,1:T(8,128)(2,1)S(1)} %get-tuple-element.474), channel_id=1, source_target_pairs={{248,0},{0,8},{8,16},{16,24},{24,32},{32,40},{40,48},{48,56},{56,6... | collective-permute-start | bytes 589832 | tf_op jit(solution)/shard_map/while/body/eval_jaxpr/ppermute | solution.py:12
  505.8 76.5 %collective-permute-start.1 = (f32[128,768]{1,0:T(8,128)S(1)}, f32[128,768]{1,0:T(8,128)S(1)}, u32[]{:S(2)}, u32[]{:S(2)}) collective-permute-start(f32[128,768]{1,0:T(8,128)S(1)} %get-tuple-element.476), channel_id=1, source_target_pairs={{248,0},{0,8},{8,16},{16,24},{24,32},{32,40},{40,48},{48,56},{56,6... | collective-permute-start | bytes 1179656 | tf_op jit(solution)/shard_map/while/body/eval_jaxpr/ppermute | solution.py:12
  582.7 57.5 %reduce-scatter.5.cloned.1.call-start = ((), (), s32[]{:S(2)}) async-start(), calls=%async_computation.3 | async-start | bytes 884736 | tf_op jit(solution)/shard_map/while/body/eval_jaxpr/reduce_scatter | solution.py:51
  582.8 18.8 %collective-permute-start = (bf16[128,3,2,128]{0,3,2,1:T(8,128)(2,1)S(1)}, bf16[128,3,2,128]{0,3,2,1:T(8,128)(2,1)S(1)}, u32[]{:S(2)}, u32[]{:S(2)}) collective-permute-start(bf16[128,3,2,128]{0,3,2,1:T(8,128)(2,1)S(1)} %get-tuple-element.474), channel_id=1, source_target_pairs={{248,0},{0,8},{8,16},{16,24},{24,32},{32,40},{40,48},{48,56},{56,6... | collective-permute-start | bytes 589832 | tf_op jit(solution)/shard_map/while/body/eval_jaxpr/ppermute | solution.py:12
  603.2 76.6 %collective-permute-start.1 = (f32[128,768]{1,0:T(8,128)S(1)}, f32[128,768]{1,0:T(8,128)S(1)}, u32[]{:S(2)}, u32[]{:S(2)}) collective-permute-start(f32[128,768]{1,0:T(8,128)S(1)} %get-tuple-element.476), channel_id=1, source_target_pairs={{248,0},{0,8},{8,16},{16,24},{24,32},{32,40},{40,48},{48,56},{56,6... | collective-permute-start | bytes 1179656 | tf_op jit(solution)/shard_map/while/body/eval_jaxpr/ppermute | solution.py:12
  680.2 57.4 %reduce-scatter.5.cloned.1.call-start = ((), (), s32[]{:S(2)}) async-start(), calls=%async_computation.3 | async-start | bytes 884736 | tf_op jit(solution)/shard_map/while/body/eval_jaxpr/reduce_scatter | solution.py:51
  680.2 18.8 %collective-permute-start = (bf16[128,3,2,128]{0,3,2,1:T(8,128)(2,1)S(1)}, bf16[128,3,2,128]{0,3,2,1:T(8,128)(2,1)S(1)}, u32[]{:S(2)}, u32[]{:S(2)}) collective-permute-start(bf16[128,3,2,128]{0,3,2,1:T(8,128)(2,1)S(1)} %get-tuple-element.474), channel_id=1, source_target_pairs={{248,0},{0,8},{8,16},{16,24},{24,32},{32,40},{40,48},{48,56},{56,6... | collective-permute-start | bytes 589832 | tf_op jit(solution)/shard_map/while/body/eval_jaxpr/ppermute | solution.py:12
  700.6 76.6 %collective-permute-start.1 = (f32[128,768]{1,0:T(8,128)S(1)}, f32[128,768]{1,0:T(8,128)S(1)}, u32[]{:S(2)}, u32[]{:S(2)}) collective-permute-start(f32[128,768]{1,0:T(8,128)S(1)} %get-tuple-element.476), channel_id=1, source_target_pairs={{248,0},{0,8},{8,16},{16,24},{24,32},{32,40},{40,48},{48,56},{56,6... | collective-permute-start | bytes 1179656 | tf_op jit(solution)/shard_map/while/body/eval_jaxpr/ppermute | solution.py:12
  777.6 57.4 %reduce-scatter.5.cloned.1.call-start = ((), (), s32[]{:S(2)}) async-start(), calls=%async_computation.3 | async-start | bytes 884736 | tf_op jit(solution)/shard_map/while/body/eval_jaxpr/reduce_scatter | solution.py:51
  777.7 18.7 %collective-permute-start = (bf16[128,3,2,128]{0,3,2,1:T(8,128)(2,1)S(1)}, bf16[128,3,2,128]{0,3,2,1:T(8,128)(2,1)S(1)}, u32[]{:S(2)}, u32[]{:S(2)}) collective-permute-start(bf16[128,3,2,128]{0,3,2,1:T(8,128)(2,1)S(1)} %get-tuple-element.474), channel_id=1, source_target_pairs={{248,0},{0,8},{8,16},{16,24},{24,32},{32,40},{40,48},{48,56},{56,6... | collective-permute-start | bytes 589832 | tf_op jit(solution)/shard_map/while/body/eval_jaxpr/ppermute | solution.py:12
  798.0 76.6 %collective-permute-start.1 = (f32[128,768]{1,0:T(8,128)S(1)}, f32[128,768]{1,0:T(8,128)S(1)}, u32[]{:S(2)}, u32[]{:S(2)}) collective-permute-start(f32[128,768]{1,0:T(8,128)S(1)} %get-tuple-element.476), channel_id=1, source_target_pairs={{248,0},{0,8},{8,16},{16,24},{24,32},{32,40},{40,48},{48,56},{56,6... | collective-permute-start | bytes 1179656 | tf_op jit(solution)/shard_map/while/body/eval_jaxpr/ppermute | solution.py:12
  875.0 57.4 %reduce-scatter.5.cloned.1.call-start = ((), (), s32[]{:S(2)}) async-start(), calls=%async_computation.3 | async-start | bytes 884736 | tf_op jit(solution)/shard_map/while/body/eval_jaxpr/reduce_scatter | solution.py:51
  875.0 18.8 %collective-permute-start = (bf16[128,3,2,128]{0,3,2,1:T(8,128)(2,1)S(1)}, bf16[128,3,2,128]{0,3,2,1:T(8,128)(2,1)S(1)}, u32[]{:S(2)}, u32[]{:S(2)}) collective-permute-start(bf16[128,3,2,128]{0,3,2,1:T(8,128)(2,1)S(1)} %get-tuple-element.474), channel_id=1, source_target_pairs={{248,0},{0,8},{8,16},{16,24},{24,32},{32,40},{40,48},{48,56},{56,6... | collective-permute-start | bytes 589832 | tf_op jit(solution)/shard_map/while/body/eval_jaxpr/ppermute | solution.py:12
  895.4 76.8 %collective-permute-start.1 = (f32[128,768]{1,0:T(8,128)S(1)}, f32[128,768]{1,0:T(8,128)S(1)}, u32[]{:S(2)}, u32[]{:S(2)}) collective-permute-start(f32[128,768]{1,0:T(8,128)S(1)} %get-tuple-element.476), channel_id=1, source_target_pairs={{248,0},{0,8},{8,16},{16,24},{24,32},{32,40},{40,48},{48,56},{56,6... | collective-permute-start | bytes 1179656 | tf_op jit(solution)/shard_map/while/body/eval_jaxpr/ppermute | solution.py:12
  972.6 57.1 %reduce-scatter.5.cloned.1.call-start = ((), (), s32[]{:S(2)}) async-start(), calls=%async_computation.3 | async-start | bytes 884736 | tf_op jit(solution)/shard_map/while/body/eval_jaxpr/reduce_scatter | solution.py:51
  972.7 18.6 %collective-permute-start = (bf16[128,3,2,128]{0,3,2,1:T(8,128)(2,1)S(1)}, bf16[128,3,2,128]{0,3,2,1:T(8,128)(2,1)S(1)}, u32[]{:S(2)}, u32[]{:S(2)}) collective-permute-start(bf16[128,3,2,128]{0,3,2,1:T(8,128)(2,1)S(1)} %get-tuple-element.474), channel_id=1, source_target_pairs={{248,0},{0,8},{8,16},{16,24},{24,32},{32,40},{40,48},{48,56},{56,6... | collective-permute-start | bytes 589832 | tf_op jit(solution)/shard_map/while/body/eval_jaxpr/ppermute | solution.py:12
  992.8 76.8 %collective-permute-start.1 = (f32[128,768]{1,0:T(8,128)S(1)}, f32[128,768]{1,0:T(8,128)S(1)}, u32[]{:S(2)}, u32[]{:S(2)}) collective-permute-start(f32[128,768]{1,0:T(8,128)S(1)} %get-tuple-element.476), channel_id=1, source_target_pairs={{248,0},{0,8},{8,16},{16,24},{24,32},{32,40},{40,48},{48,56},{56,6... | collective-permute-start | bytes 1179656 | tf_op jit(solution)/shard_map/while/body/eval_jaxpr/ppermute | solution.py:12
  1070.0 57.2 %reduce-scatter.5.cloned.1.call-start = ((), (), s32[]{:S(2)}) async-start(), calls=%async_computation.3 | async-start | bytes 884736 | tf_op jit(solution)/shard_map/while/body/eval_jaxpr/reduce_scatter | solution.py:51
  1070.1 18.6 %collective-permute-start = (bf16[128,3,2,128]{0,3,2,1:T(8,128)(2,1)S(1)}, bf16[128,3,2,128]{0,3,2,1:T(8,128)(2,1)S(1)}, u32[]{:S(2)}, u32[]{:S(2)}) collective-permute-start(bf16[128,3,2,128]{0,3,2,1:T(8,128)(2,1)S(1)} %get-tuple-element.474), channel_id=1, source_target_pairs={{248,0},{0,8},{8,16},{16,24},{24,32},{32,40},{40,48},{48,56},{56,6... | collective-permute-start | bytes 589832 | tf_op jit(solution)/shard_map/while/body/eval_jaxpr/ppermute | solution.py:12
  1090.3 76.7 %collective-permute-start.1 = (f32[128,768]{1,0:T(8,128)S(1)}, f32[128,768]{1,0:T(8,128)S(1)}, u32[]{:S(2)}, u32[]{:S(2)}) collective-permute-start(f32[128,768]{1,0:T(8,128)S(1)} %get-tuple-element.476), channel_id=1, source_target_pairs={{248,0},{0,8},{8,16},{16,24},{24,32},{32,40},{40,48},{48,56},{56,6... | collective-permute-start | bytes 1179656 | tf_op jit(solution)/shard_map/while/body/eval_jaxpr/ppermute | solution.py:12
  1167.4 57.2 %reduce-scatter.5.cloned.1.call-start = ((), (), s32[]{:S(2)}) async-start(), calls=%async_computation.3 | async-start | bytes 884736 | tf_op jit(solution)/shard_map/while/body/eval_jaxpr/reduce_scatter | solution.py:51
  1167.4 18.5 %collective-permute-start = (bf16[128,3,2,128]{0,3,2,1:T(8,128)(2,1)S(1)}, bf16[128,3,2,128]{0,3,2,1:T(8,128)(2,1)S(1)}, u32[]{:S(2)}, u32[]{:S(2)}) collective-permute-start(bf16[128,3,2,128]{0,3,2,1:T(8,128)(2,1)S(1)} %get-tuple-element.474), channel_id=1, source_target_pairs={{248,0},{0,8},{8,16},{16,24},{24,32},{32,40},{40,48},{48,56},{56,6... | collective-permute-start | bytes 589832 | tf_op jit(solution)/shard_map/while/body/eval_jaxpr/ppermute | solution.py:12
  1187.6 76.6 %collective-permute-start.1 = (f32[128,768]{1,0:T(8,128)S(1)}, f32[128,768]{1,0:T(8,128)S(1)}, u32[]{:S(2)}, u32[]{:S(2)}) collective-permute-start(f32[128,768]{1,0:T(8,128)S(1)} %get-tuple-element.476), channel_id=1, source_target_pairs={{248,0},{0,8},{8,16},{16,24},{24,32},{32,40},{40,48},{48,56},{56,6... | collective-permute-start | bytes 1179656 | tf_op jit(solution)/shard_map/while/body/eval_jaxpr/ppermute | solution.py:12
  1264.5 57.5 %reduce-scatter.5.cloned.1.call-start = ((), (), s32[]{:S(2)}) async-start(), calls=%async_computation.3 | async-start | bytes 884736 | tf_op jit(solution)/shard_map/while/body/eval_jaxpr/reduce_scatter | solution.py:51
  1264.6 18.9 %collective-permute-start = (bf16[128,3,2,128]{0,3,2,1:T(8,128)(2,1)S(1)}, bf16[128,3,2,128]{0,3,2,1:T(8,128)(2,1)S(1)}, u32[]{:S(2)}, u32[]{:S(2)}) collective-permute-start(bf16[128,3,2,128]{0,3,2,1:T(8,128)(2,1)S(1)} %get-tuple-element.474), channel_id=1, source_target_pairs={{248,0},{0,8},{8,16},{16,24},{24,32},{32,40},{40,48},{48,56},{56,6... | collective-permute-start | bytes 589832 | tf_op jit(solution)/shard_map/while/body/eval_jaxpr/ppermute | solution.py:12
  1285.0 76.9 %collective-permute-start.1 = (f32[128,768]{1,0:T(8,128)S(1)}, f32[128,768]{1,0:T(8,128)S(1)}, u32[]{:S(2)}, u32[]{:S(2)}) collective-permute-start(f32[128,768]{1,0:T(8,128)S(1)} %get-tuple-element.476), channel_id=1, source_target_pairs={{248,0},{0,8},{8,16},{16,24},{24,32},{32,40},{40,48},{48,56},{56,6... | collective-permute-start | bytes 1179656 | tf_op jit(solution)/shard_map/while/body/eval_jaxpr/ppermute | solution.py:12
  1362.3 57.1 %reduce-scatter.5.cloned.1.call-start = ((), (), s32[]{:S(2)}) async-start(), calls=%async_computation.3 | async-start | bytes 884736 | tf_op jit(solution)/shard_map/while/body/eval_jaxpr/reduce_scatter | solution.py:51
  1362.3 18.5 %collective-permute-start = (bf16[128,3,2,128]{0,3,2,1:T(8,128)(2,1)S(1)}, bf16[128,3,2,128]{0,3,2,1:T(8,128)(2,1)S(1)}, u32[]{:S(2)}, u32[]{:S(2)}) collective-permute-start(bf16[128,3,2,128]{0,3,2,1:T(8,128)(2,1)S(1)} %get-tuple-element.474), channel_id=1, source_target_pairs={{248,0},{0,8},{8,16},{16,24},{24,32},{32,40},{40,48},{48,56},{56,6... | collective-permute-start | bytes 589832 | tf_op jit(solution)/shard_map/while/body/eval_jaxpr/ppermute | solution.py:12
  1382.4 76.6 %collective-permute-start.1 = (f32[128,768]{1,0:T(8,128)S(1)}, f32[128,768]{1,0:T(8,128)S(1)}, u32[]{:S(2)}, u32[]{:S(2)}) collective-permute-start(f32[128,768]{1,0:T(8,128)S(1)} %get-tuple-element.476), channel_id=1, source_target_pairs={{248,0},{0,8},{8,16},{16,24},{24,32},{32,40},{40,48},{48,56},{56,6... | collective-permute-start | bytes 1179656 | tf_op jit(solution)/shard_map/while/body/eval_jaxpr/ppermute | solution.py:12
  1459.4 57.5 %reduce-scatter.5.cloned.1.call-start = ((), (), s32[]{:S(2)}) async-start(), calls=%async_computation.3 | async-start | bytes 884736 | tf_op jit(solution)/shard_map/while/body/eval_jaxpr/reduce_scatter | solution.py:51
  1459.4 18.8 %collective-permute-start = (bf16[128,3,2,128]{0,3,2,1:T(8,128)(2,1)S(1)}, bf16[128,3,2,128]{0,3,2,1:T(8,128)(2,1)S(1)}, u32[]{:S(2)}, u32[]{:S(2)}) collective-permute-start(bf16[128,3,2,128]{0,3,2,1:T(8,128)(2,1)S(1)} %get-tuple-element.474), channel_id=1, source_target_pairs={{248,0},{0,8},{8,16},{16,24},{24,32},{32,40},{40,48},{48,56},{56,6... | collective-permute-start | bytes 589832 | tf_op jit(solution)/shard_map/while/body/eval_jaxpr/ppermute | solution.py:12
  1479.8 76.8 %collective-permute-start.1 = (f32[128,768]{1,0:T(8,128)S(1)}, f32[128,768]{1,0:T(8,128)S(1)}, u32[]{:S(2)}, u32[]{:S(2)}) collective-permute-start(f32[128,768]{1,0:T(8,128)S(1)} %get-tuple-element.476), channel_id=1, source_target_pairs={{248,0},{0,8},{8,16},{16,24},{24,32},{32,40},{40,48},{48,56},{56,6... | collective-permute-start | bytes 1179656 | tf_op jit(solution)/shard_map/while/body/eval_jaxpr/ppermute | solution.py:12
  1557.0 57.2 %reduce-scatter.5.cloned.1.call-start = ((), (), s32[]{:S(2)}) async-start(), calls=%async_computation.3 | async-start | bytes 884736 | tf_op jit(solution)/shard_map/while/body/eval_jaxpr/reduce_scatter | solution.py:51
  1557.1 18.6 %collective-permute-start = (bf16[128,3,2,128]{0,3,2,1:T(8,128)(2,1)S(1)}, bf16[128,3,2,128]{0,3,2,1:T(8,128)(2,1)S(1)}, u32[]{:S(2)}, u32[]{:S(2)}) collective-permute-start(bf16[128,3,2,128]{0,3,2,1:T(8,128)(2,1)S(1)} %get-tuple-element.474), channel_id=1, source_target_pairs={{248,0},{0,8},{8,16},{16,24},{24,32},{32,40},{40,48},{48,56},{56,6... | collective-permute-start | bytes 589832 | tf_op jit(solution)/shard_map/while/body/eval_jaxpr/ppermute | solution.py:12
  1577.3 76.6 %collective-permute-start.1 = (f32[128,768]{1,0:T(8,128)S(1)}, f32[128,768]{1,0:T(8,128)S(1)}, u32[]{:S(2)}, u32[]{:S(2)}) collective-permute-start(f32[128,768]{1,0:T(8,128)S(1)} %get-tuple-element.476), channel_id=1, source_target_pairs={{248,0},{0,8},{8,16},{16,24},{24,32},{32,40},{40,48},{48,56},{56,6... | collective-permute-start | bytes 1179656 | tf_op jit(solution)/shard_map/while/body/eval_jaxpr/ppermute | solution.py:12
  (3 other events, 28.2 us)
Sparse Core Ops, SparseCore 0:
  16.2 39.5 reduce-scatter.2
  116.3 36.7 reduce-scatter.4
  213.8 36.7 reduce-scatter.4
  311.1 36.8 reduce-scatter.4
  408.5 36.8 reduce-scatter.4
  505.9 36.8 reduce-scatter.4
  603.3 36.8 reduce-scatter.4
  700.7 36.8 reduce-scatter.4
  798.1 36.8 reduce-scatter.4
  895.5 36.8 reduce-scatter.4
  993.0 36.7 reduce-scatter.4
  1090.4 36.7 reduce-scatter.4
  1187.7 36.8 reduce-scatter.4
  1285.2 36.7 reduce-scatter.4
  1382.6 36.8 reduce-scatter.4
  1480.0 36.8 reduce-scatter.4
  1577.4 36.7 reduce-scatter.4
where the time goes:
time: 1690 us; the launch traced here: 1670 us
  blocking collectives  618 us (37%)
  waiting for transfers between devices  603 us (36%)
  starting transfers between devices  301 us (18%)
  other arithmetic  53.8 us (3%)
  matrix products  48.1 us (3%)
  local copies, waits for them, and re-layouts  30.5 us (2%)
    reduce_scatter x17, waiting for transfers between devices, forward(): lax.psum_scatter(jnp.einsum('prf,rft->tp', cross, local_table, preferred_...  590 us
    all_gather x17, blocking collectives, correlate(): spectral = back(lax.all_gather(adjoint, 'lag', axis=1, tiled=True))  383 us
    ppermute x33, starting transfers between devices, from_behind(): return lax.ppermute(block, axis, route)  300 us
    psum x17, blocking collectives, correlate(): lax.psum(jnp.sum(weight[None, :] * lagged * lagged, axis=1) / lag_total,...  235 us
  transfers between devices with their start and end apart: 50, of which 34 were waited for; matrix products, arithmetic and copies ran while one was open for 5% of the time, Pallas kernels for 0%

commit v1 on v0

v1 whole, which is shorter than its diff:
```python
import math

import jax
import jax.numpy as jnp
import numpy as np
from jax import lax
from jax.experimental import pallas as pl
from jax.experimental.pallas import tpu as pltpu
from jax.sharding import Mesh
from jax.sharding import PartitionSpec as P

BF = jnp.bfloat16
F32 = jnp.float32
PLANE = ("yh", "c", "yl", "x")
QUAD = ("yh", "c")
COLS = 8
HALO = (0, 1, 2, -2)
PLACES = {0: (0, 0), 1: (1, 0), 2: (2, 0), 3: (1, 3), 4: (2, 3), 5: (3, 1), 6: (3, 0), 7: (0, 1)}
STEPS = 17
SLOTS = 96
KROWS = 24
NONE = 1024.0


def operator_parts(freq_total):
    lags = 2 * freq_total
    order = np.array(
        [(s % 8) * (freq_total // 8) + (s // 8) * (freq_total // 32) + f for s in range(32) for f in range(freq_total // 32)]
    )
    k = np.arange(-freq_total, 2 * freq_total)
    with np.errstate(divide="ignore"):
        sines = np.where(k == 0, 0.0, -1.5 / np.tan(np.pi * np.where(k == 0, 1, k) / lags))
    f = order[:, None]
    h = order[None, :]
    couple = -(sines[h + f + freq_total] + sines[h - f + freq_total]) / lags
    top = lags + 1.5 * (lags - 1)
    real = np.where(order == 0, 2 * top + 3.0, top - 1.5 + 3.0) / lags
    imag = np.where(order == 0, 0.0, top + 1.5) / lags
    return couple, real, imag, -3.0 / lags


def block_table():
    table = np.zeros((COLS, STEPS, 4, 2), np.int32)
    holder = np.zeros((2, KROWS, 128), np.float32)
    for z in range(COLS):
        for k in range(STEPS):
            for q in range(4):
                yh, c = q // 2, q % 2
                gap = -((c - k) // 2) % COLS
                i, j = PLACES[gap]
                other = (16 * yh + 2 * ((z + HALO[i]) % COLS) + c - k) % 32
                assert (z + HALO[j]) % COLS == other % 16 // 2
                table[z, k, q, 0] = i * 4 + q
                table[z, k, q, 1] = j * 4 + other // 16 * 2 + other % 2
                holder[c, k, :] = i
    return table.reshape(-1), holder


def one_hot(row):
    rows = lax.broadcasted_iota(jnp.int32, (256, 128), 0)
    return (rows == row).astype(F32).astype(BF)


def gather(held, first, second, pick):
    both = jnp.concatenate([held[first], held[second]], axis=1)
    return jnp.dot(both, pick, preferred_element_type=F32)


def cross_body(z_ref, tab_ref, holder_ref, g0, g1, g2, g3, out_ref, idx_ref, held):
    lane = lax.broadcasted_iota(jnp.int32, (KROWS, 128), 1)
    for i, g in enumerate((g0, g1, g2, g3)):
        held[4 * i : 4 * i + 4] = g[:, 0:192, :]
    for side in range(2):
        rolled = []
        for q in range(4):
            where = holder_ref[q % 2]
            lo = 192 + KROWS * side
            rows = jnp.zeros((KROWS, 128), F32)
            for i, g in enumerate((g0, g1, g2, g3)):
                rows = jnp.where(where == float(i), g[q, lo : lo + KROWS, :].astype(F32), rows)
            rows = rows.astype(jnp.int32)
            rolled.append(rows if q == 0 else pltpu.roll(rows, 128 - 32 * q, 1))
        for a in range(3):
            idx_ref[side, a] = jnp.where(lane < 96 - 32 * a, rolled[a], rolled[a + 1] + 128)
    base = z_ref[0] * (STEPS * 8)

    def step(k, carry):
        for a in range(3):
            tile = 3 * k + a
            at = base + k * 8 + a * 2
            u = gather(held, tab_ref[at], tab_ref[at + 2], one_hot(idx_ref[0, a, pl.ds(k, 1), :]))
            v = gather(held, tab_ref[at + 1], tab_ref[at + 3], one_hot(idx_ref[1, a, pl.ds(k, 1), :]))
            real = jnp.zeros((32, 128), F32)
            imag = jnp.zeros((32, 128), F32)
            for c in range(3):
                ur, ui = u[64 * c : 64 * c + 32], u[64 * c + 32 : 64 * c + 64]
                vr, vi = v[64 * c : 64 * c + 32], v[64 * c + 32 : 64 * c + 64]
                real += ur * vr + ui * vi
                imag += ui * vr - ur * vi
            part = jnp.concatenate([real, imag], 0).astype(BF)
            out_ref[tile // 2, :, pl.ds(pl.multiple_of(tile % 2 * 128, 128), 128)] = part
        return carry

    lax.fori_loop(0, STEPS, step, 0)
    for tile in range(3 * STEPS, 64):
        out_ref[tile // 2, :, tile % 2 * 128 : tile % 2 * 128 + 128] = jnp.zeros((64, 128), BF)


def spectral_body(cross_ref, couple_ref, couple_t_ref, diag_ref, out_ref):
    cross = cross_ref[...]
    lags = 2.0 * couple_ref.shape[0]
    size = couple_ref.shape[0]
    c0 = cross[:, 0:32, :].reshape(size, 256)
    c1 = cross[:, 32:64, :].reshape(size, 256)
    f0 = c0.astype(F32)
    f1 = c1.astype(F32)
    y0 = jnp.dot(couple_ref[...], c1, preferred_element_type=F32)
    y0 += diag_ref[:, 0:1] * f0 + (-3.0 / lags) * jnp.sum(f0, axis=0, keepdims=True)
    y1 = jnp.dot(couple_t_ref[...], c0, preferred_element_type=F32) + diag_ref[:, 1:2] * f1
    energy = jnp.sum(y0 * f0 + y1 * f1, axis=0, keepdims=True) / lags
    scale = 1.0 / jnp.sqrt(energy + 1e-5)
    out_ref[:, 0:32, :] = (y0 * scale).astype(BF).reshape(32, 32, 256)
    out_ref[:, 32:64, :] = (y1 * scale).astype(BF).reshape(32, 32, 256)


def sums_body(z_ref, tab_ref, idx_ref, g0, g1, g2, g3, spec_ref, o0, o1, o2, o3, held, acc):
    for i, g in enumerate((g0, g1, g2, g3)):
        held[4 * i : 4 * i + 4] = g[:, 0:192, :]
    acc[...] = jnp.zeros(acc.shape, F32)
    base = z_ref[0] * (STEPS * 8)
    dims = (((1,), (1,)), ((), ()))

    def step(k, carry):
        for a in range(3):
            tile = 3 * k + a
            at = base + k * 8 + a * 2
            ua, va, ub, vb = (tab_ref[at + n] for n in range(4))
            pick_u = one_hot(idx_ref[0, a, pl.ds(k, 1), :])
            pick_v = one_hot(idx_ref[1, a, pl.ds(k, 1), :])
            u = gather(held, ua, ub, pick_u)
            v = gather(held, va, vb, pick_v)
            spec = spec_ref[tile // 2, :, pl.ds(pl.multiple_of(tile % 2 * 128, 128), 128)].astype(F32)
            a0 = spec[0:32]
            a1 = spec[32:64]
            near = []
            far = []
            for c in range(3):
                ur, ui = u[64 * c : 64 * c + 32], u[64 * c + 32 : 64 * c + 64]
                vr, vi = v[64 * c : 64 * c + 32], v[64 * c + 32 : 64 * c + 64]
                near += [a0 * vr - a1 * vi, a0 * vi + a1 * vr]
                far += [a0 * ur + a1 * ui, a0 * ui - a1 * ur]
            near = jnp.concatenate(near, 0).astype(BF)
            far = jnp.concatenate(far, 0).astype(BF)
            to_u = lax.dot_general(near, pick_u, dims, preferred_element_type=F32)
            to_v = lax.dot_general(far, pick_v, dims, preferred_element_type=F32)
            acc[ua] += to_u[:, 0:128]
            acc[ub] += to_u[:, 128:256]
            acc[va] += to_v[:, 0:128]
            acc[vb] += to_v[:, 128:256]
        return carry

    lax.fori_loop(0, STEPS, step, 0)
    o0[...] = acc[0:4]
    for i, o in enumerate((o1, o2, o3)):
        o[...] = acc[4 * i + 4 : 4 * i + 8].astype(BF)


def whiten(spectra, band, first_freq):
    values = spectra.astype(F32).transpose(1, 2, 3, 0)
    meansq = jnp.mean(values * values, axis=(0, 1))
    freq = (first_freq + jnp.arange(values.shape[2], dtype=jnp.int32))[:, None]
    inside = (freq >= band[None, :, 0]) & (freq < band[None, :, 1])
    factor = jnp.where(inside, 1.0 / jnp.sqrt(jnp.maximum(meansq, 0.25)), 0.0)
    return (values * factor).astype(BF)


def on_device(spectra, band, pair_lists, pair_counts):
    stations, comps, parts, bins = spectra.shape
    freq_total = bins * 8
    params = pltpu.CompilerParams(vmem_limit_bytes=56 << 20)
    vmem = pl.BlockSpec(memory_space=pltpu.VMEM)
    smem = pl.BlockSpec(memory_space=pltpu.SMEM)
    zi = lax.axis_index("z").astype(jnp.int32).reshape(1)
    lane = lax.axis_index(("yl", "x"))
    table, holder = block_table()
    table = jnp.asarray(table)

    white = whiten(spectra, band, lane * bins)
    white = white.reshape(comps * parts, 4, bins // 4, stations).transpose(1, 0, 2, 3)
    white = white.reshape(4, comps * parts * bins // 4, stations)
    used = jnp.arange(SLOTS, dtype=jnp.int32)[None, None, :] < pair_counts[0][:, None, None]
    lists = jnp.where(used, pair_lists[0].transpose(0, 2, 1), int(NONE)).astype(BF)
    lists = jnp.pad(lists, ((0, KROWS - STEPS), (0, 0), (0, 128 - SLOTS)), constant_values=NONE)
    lists = lists.transpose(1, 0, 2).reshape(1, 2 * KROWS, 128)
    block = jnp.concatenate([white, jnp.broadcast_to(lists, (4, 2 * KROWS, 128))], 1)
    own = lax.all_to_all(block, QUAD, 0, 0, tiled=True)
    groups = [own]
    for d in HALO[1:]:
        groups.append(lax.ppermute(own, "z", [((z + d) % COLS, z) for z in range(COLS)]))

    cross, index = pl.pallas_call(
        cross_body,
        in_specs=[smem, smem] + [vmem] * 5,
        out_specs=[vmem, vmem],
        out_shape=[
            jax.ShapeDtypeStruct((32, 64, 256), BF),
            jax.ShapeDtypeStruct((2, 3, KROWS, 128), jnp.int32),
        ],
        scratch_shapes=[pltpu.VMEM((16, 192, 128), BF)],
        compiler_params=params,
        name="cross",
    )(zi, table, jnp.asarray(holder), *groups)
    cross = lax.all_to_all(cross, PLANE, 0, 0, tiled=True)

    couple, real, imag, _ = operator_parts(freq_total)
    spectral = pl.pallas_call(
        spectral_body,
        in_specs=[vmem] * 4,
        out_specs=vmem,
        out_shape=jax.ShapeDtypeStruct((32, 64, 256), BF),
        compiler_params=params,
        name="spectral",
    )(
        cross,
        jnp.asarray(couple.astype(np.float32)).astype(BF),
        jnp.asarray(couple.T.astype(np.float32)).astype(BF),
        jnp.asarray(np.stack([real, imag], 1).astype(np.float32)),
    )
    spectral = lax.all_to_all(spectral, PLANE, 0, 0, tiled=True)

    sums = pl.pallas_call(
        sums_body,
        in_specs=[smem, smem] + [vmem] * 6,
        out_specs=[vmem] * 4,
        out_shape=[jax.ShapeDtypeStruct((4, 192, 128), F32)] + [jax.ShapeDtypeStruct((4, 192, 128), BF)] * 3,
        scratch_shapes=[pltpu.VMEM((16, 192, 128), BF), pltpu.VMEM((16, 192, 128), F32)],
        compiler_params=params,
        name="sums",
    )(zi, table, index, *groups, spectral)
    total = sums[0]
    for d, part in zip(HALO[1:], sums[1:]):
        back = lax.ppermute(part, "z", [(z, (z + d) % COLS) for z in range(COLS)])
        total = total + back.astype(F32)
    total = lax.all_to_all(total.astype(BF), QUAD, 0, 0, tiled=True)
    total = total.reshape(4, comps, parts, bins // 4, stations).transpose(4, 1, 2, 0, 3)
    return total.reshape(stations, comps, parts, bins).astype(F32) / math.sqrt(SLOTS)


def solution(mesh):
    fine = Mesh(mesh.devices.reshape(2, 8, 2, 2, 4), ("yh", "z", "c", "yl", "x"))
    blk = ("yh", "z", "c")
    lag = ("yl", "x")
    in_specs = (P(blk, None, None, lag), P(blk, None), P(blk, None, None, None), P(blk, None))
    return jax.shard_map(
        on_device, mesh=fine, in_specs=in_specs, out_specs=P(blk, None, None, lag), check_vma=False
    )
```

time: 1690 us -> 143 us (0.08); the launches traced: 1670 us -> 142 us
  waiting for transfers between devices: 603 us -> 26.9 us
  blocking collectives: 618 us -> 66.3 us
  starting transfers between devices: 301 us -> 12.3 us
  other arithmetic: 53.8 us -> 2.79 us
  matrix products: 48.1 us -> 0 us
  Pallas kernels: 0 us -> 30.5 us
  local copies, waits for them, and re-layouts: 30.5 us -> 3.53 us
    reduce_scatter x17 -> x0, waiting for transfers between devices: 590 us -> none  [forward(): lax.psum_scatter(jnp.einsum('prf,rft->tp', cross, local_table, preferred_...]
    all_gather x17 -> x0, blocking collectives: 383 us -> none  [correlate(): spectral = back(lax.all_gather(adjoint, 'lag', axis=1, tiled=True))]
    ppermute x33 -> x6, starting transfers between devices: 300 us -> 12.3 us  [the longest x3 7.94 us: on_device(): lax.ppermute(own, 'z', [((z + d) % COLS, z) for z in range(COLS)])]
    psum x17 -> x0, blocking collectives: 235 us -> none  [correlate(): lax.psum(jnp.sum(weight[None, :] * lagged * lagged, axis=1) / lag_total,...]
    all_to_all x0 -> x4, blocking collectives: none -> 66.3 us  [the longest x1 23.4 us: on_device(): cross = lax.all_to_all(cross, PLANE, 0, 0, tiled=True)]
    dot_general x102 -> x0, matrix products: 48.1 us -> none  [the longest x17 20.3 us: forward(): jnp.einsum('prf,rft->tp', cross, local_table, preferred_element_type=jnp....]
    pallas_call x0 -> x3, Pallas kernels: none -> 30.5 us  [the longest x1 17.4 us: on_device(): pl.pallas_call(sums_body, in_specs=[smem, smem] + [vmem] * 6, out_specs=[...]
    convert_element_type x35 -> x3, other arithmetic: 27.1 us -> 1.88 us  [the longest x1 1.1 us: on_device(): total = lax.all_to_all(total.astype(BF), QUAD, 0, 0, tiled=True)]
  transfers between devices with their start and end apart: 50 -> 6, of which waited for: 34 -> 6; matrix products, arithmetic and copies ran while one was open for 5% -> 0% of each run, Pallas kernels for 0% -> 0%
where the time goes in v1:
time: 143 us; the launch traced here: 142 us
  blocking collectives  66.3 us (46%)
  Pallas kernels  30.5 us (21%)
  waiting for transfers between devices  26.9 us (19%)
  starting transfers between devices  12.3 us (9%)
  local copies, waits for them, and re-layouts  3.53 us (2%)
  other arithmetic  2.79 us (2%)
    all_to_all x1, blocking collectives, on_device(): cross = lax.all_to_all(cross, PLANE, 0, 0, tiled=True)  23.4 us
    all_to_all x1, blocking collectives, on_device(): spectral = lax.all_to_all(spectral, PLANE, 0, 0, tiled=True)  21.8 us
    pallas_call x1, Pallas kernels, on_device(): pl.pallas_call(sums_body, in_specs=[smem, smem] + [vmem] * 6, out_specs=[...  17.4 us
    ppermute x3, waiting for transfers between devices, on_device(): lax.ppermute(own, 'z', [((z + d) % COLS, z) for z in range(COLS)])  14.9 us
    all_to_all x1, blocking collectives, on_device(): own = lax.all_to_all(block, QUAD, 0, 0, tiled=True)  12.1 us
    ppermute x3, waiting for transfers between devices, on_device(): back = lax.ppermute(part, 'z', [(z, (z + d) % COLS) for z in range(COLS)])  12 us
    all_to_all x1, blocking collectives, on_device(): total = lax.all_to_all(total.astype(BF), QUAD, 0, 0, tiled=True)  8.95 us
    ppermute x3, starting transfers between devices, on_device(): lax.ppermute(own, 'z', [((z + d) % COLS, z) for z in range(COLS)])  7.94 us
  transfers between devices with their start and end apart: 6, of which 6 were waited for; matrix products, arithmetic and copies ran while one was open for 0% of the time, Pallas kernels for 0%

profile of v1, /device:TPU:1, one launch (start us, length us, event | category | flops | bytes accessed | tf_op | source)
XLA Modules:
  0.0 142.4 jit_solution(14505331817881491051)
XLA Ops:
  0.0 0.8 slice_bitcast_fusion.1
  0.8 0.7 iota_compare_fusion
  1.5 1.1 copy.12
  2.6 0.1 rsqrt_select_fusion
  2.8 0.7 fusion.3
  3.6 12.1 %all_to_all.20.g0 = bf16[4,240,128]{2,1,0:T(8,128)(2,1)S(1)} all-to-all(bf16[4,240,128]{2,1,0:T(8,128)(2,1)S(1)} %pad_maximum_fusion), channel_id=1, replica_groups=mesh['yh'=2,'z'=8,'c'=2,'yl'=2,'x'=4] {'yh','c'}, dimensions={0} | all-to-all | bytes 491520 | tf_op jit(solution)/shard_map/all_to_all | solution.py:196
  15.7 0.0 copy-start
  15.7 3.0 %collective-permute-start.2 = (bf16[4,240,128]{2,1,0:T(8,128)(2,1)S(1)}, bf16[4,240,128]{2,1,0:T(8,128)(2,1)S(1)}, u32[]{:S(2)}, u32[]{:S(2)}) collective-permute-start(bf16[4,240,128]{2,1,0:T(8,128)(2,1)S(1)} %all_to_all.20.g0), channel_id=1, source_target_pairs={{96,0},{112,16},{0,32},{16,48},{32,64},{48,80},{64,96},{80,112},{9... | collective-permute-start | bytes 737288 | tf_op jit(solution)/shard_map/ppermute | solution.py:199
  18.7 3.0 %collective-permute-start.1 = (bf16[4,240,128]{2,1,0:T(8,128)(2,1)S(1)}, bf16[4,240,128]{2,1,0:T(8,128)(2,1)S(1)}, u32[]{:S(2)}, u32[]{:S(2)}) collective-permute-start(bf16[4,240,128]{2,1,0:T(8,128)(2,1)S(1)} %all_to_all.20.g0), channel_id=1, source_target_pairs={{32,0},{48,16},{64,32},{80,48},{96,64},{112,80},{0,96},{16,112},{3... | collective-permute-start | bytes 737288 | tf_op jit(solution)/shard_map/ppermute | solution.py:199
  21.8 1.9 %collective-permute-start = (bf16[4,240,128]{2,1,0:T(8,128)(2,1)S(1)}, bf16[4,240,128]{2,1,0:T(8,128)(2,1)S(1)}, u32[]{:S(2)}, u32[]{:S(2)}) collective-permute-start(bf16[4,240,128]{2,1,0:T(8,128)(2,1)S(1)} %all_to_all.20.g0), channel_id=1, source_target_pairs={{16,0},{32,16},{48,32},{64,48},{80,64},{96,80},{112,96},{0,112},{1... | collective-permute-start | bytes 737288 | tf_op jit(solution)/shard_map/ppermute | solution.py:199
  23.7 5.0 %collective-permute-done.2.g3 = bf16[4,240,128]{2,1,0:T(8,128)(2,1)S(1)} collective-permute-done((bf16[4,240,128]{2,1,0:T(8,128)(2,1)S(1)}, bf16[4,240,128]{2,1,0:T(8,128)(2,1)S(1)}, u32[]{:S(2)}, u32[]{:S(2)}) %collective-permute-start.2) | collective-permute-done | bytes 245792 | tf_op jit(solution)/shard_map/ppermute | solution.py:199
  28.7 0.0 copy-start.1
  28.7 5.4 %collective-permute-done.1.g2 = bf16[4,240,128]{2,1,0:T(8,128)(2,1)S(1)} collective-permute-done((bf16[4,240,128]{2,1,0:T(8,128)(2,1)S(1)}, bf16[4,240,128]{2,1,0:T(8,128)(2,1)S(1)}, u32[]{:S(2)}, u32[]{:S(2)}) %collective-permute-start.1) | collective-permute-done | bytes 245792 | tf_op jit(solution)/shard_map/ppermute | solution.py:199
  34.1 0.0 copy-start.2
  34.1 4.5 %collective-permute-done.g1 = bf16[4,240,128]{2,1,0:T(8,128)(2,1)S(1)} collective-permute-done((bf16[4,240,128]{2,1,0:T(8,128)(2,1)S(1)}, bf16[4,240,128]{2,1,0:T(8,128)(2,1)S(1)}, u32[]{:S(2)}, u32[]{:S(2)}) %collective-permute-start) | collective-permute-done | bytes 245792 | tf_op jit(solution)/shard_map/ppermute | solution.py:199
  38.6 0.0 copy-start.3
  38.6 0.0 copy-done
  38.6 0.0 copy-done.1
  38.6 0.0 copy-done.2
  38.6 0.7 copy-done.3
  39.3 7.8 %cross.1 = (bf16[32,64,256]{2,1,0:T(8,128)(2,1)}, s32[2,3,24,128]{3,2,1,0:T(8,128)}) custom-call(s32[1]{0:T(128)} %bitcast.z_ref, s32[1088]{0:T(1024)} %constant.45.clone.tab_ref, f32[2,24,128]{2,1,0:T(8,128)} %constant.46.clone.holder_ref, bf16[4,240,128]{2,1,0:T(8,128)(2,1)} %copy-done, bf16[4,240,128]{2,1,0:T(8,128)(2,1)} %copy-done.3, ...), custom_call_target="tpu_custom_call" | custom-call | tf_op jit(solution)/shard_map/cross/pallas_call | solution.py:201
  47.1 23.4 %all_to_all.21.cross_ref = bf16[32,64,256]{2,1,0:T(8,128)(2,1)} all-to-all(bf16[32,64,256]{2,1,0:T(8,128)(2,1)} %get-tuple-element.12), channel_id=1, replica_groups=mesh['yh'=2,'z'=8,'c'=2,'yl'=2,'x'=4] {'yh','c','yl','x'}, dimensions={0} | all-to-all | bytes 2097152 | tf_op jit(solution)/shard_map/all_to_all | solution.py:213
  70.5 5.3 %spectral.1 = bf16[32,64,256]{2,1,0:T(8,128)(2,1)} custom-call(bf16[32,64,256]{2,1,0:T(8,128)(2,1)} %all_to_all.21.cross_ref, bf16[1024,1024]{1,0:T(8,128)(2,1)} %constant.54.couple_ref, bf16[1024,1024]{1,0:T(8,128)(2,1)} %constant.55.couple_t_ref, f32[1024,2]{1,0:T(8,128)} %constant.49.clone.diag_ref), custom_call_target="tpu_custom_call" | custom-call | tf_op jit(solution)/shard_map/spectral/pallas_call | solution.py:216
  75.8 21.8 %all_to_all.22.spec_ref = bf16[32,64,256]{2,1,0:T(8,128)(2,1)} all-to-all(bf16[32,64,256]{2,1,0:T(8,128)(2,1)} %spectral.1), channel_id=1, replica_groups=mesh['yh'=2,'z'=8,'c'=2,'yl'=2,'x'=4] {'yh','c','yl','x'}, dimensions={0} | all-to-all | bytes 2097152 | tf_op jit(solution)/shard_map/all_to_all | solution.py:229
  97.6 17.4 %sums.1 = (f32[4,192,128]{2,1,0:T(8,128)}, bf16[4,192,128]{2,1,0:T(8,128)(2,1)}, bf16[4,192,128]{2,1,0:T(8,128)(2,1)}, bf16[4,192,128]{2,1,0:T(8,128)(2,1)}) custom-call(s32[1]{0:T(128)} %bitcast.z_ref, s32[1088]{0:T(1024)} %constant.45.clone.tab_ref, s32[2,3,24,128]{3,2,1,0:T(8,128)} %get-tuple-element.11.idx_ref, bf16[4,240,128]{2,1,0:T(8,128)(2,1)} %copy-done, ...), custom_call_target="tpu_custom_call" | custom-call | tf_op jit(solution)/shard_map/sums/pallas_call | solution.py:231
  115.0 0.8 collective-permute-start.3
  115.8 3.5 %collective-permute-start.4 = (bf16[4,192,128]{2,1,0:T(8,128)(2,1)}, bf16[4,192,128]{2,1,0:T(8,128)(2,1)S(1)}, u32[]{:S(2)}, u32[]{:S(2)}) collective-permute-start(bf16[4,192,128]{2,1,0:T(8,128)(2,1)} %get-tuple-element.15), channel_id=1, source_target_pairs={{0,32},{16,48},{32,64},{48,80},{64,96},{80,112},{96,0},{112,16},{1... | collective-permute-start | bytes 589832 | tf_op jit(solution)/shard_map/ppermute | solution.py:242
  119.3 0.0 collective-permute-start.5
  119.4 3.5 %collective-permute-done.3 = bf16[4,192,128]{2,1,0:T(8,128)(2,1)S(1)} collective-permute-done((bf16[4,192,128]{2,1,0:T(8,128)(2,1)}, bf16[4,192,128]{2,1,0:T(8,128)(2,1)S(1)}, u32[]{:S(2)}, u32[]{:S(2)}) %collective-permute-start.3) | collective-permute-done | bytes 196640 | tf_op jit(solution)/shard_map/ppermute | solution.py:242
  122.9 7.6 %collective-permute-done.4 = bf16[4,192,128]{2,1,0:T(8,128)(2,1)S(1)} collective-permute-done((bf16[4,192,128]{2,1,0:T(8,128)(2,1)}, bf16[4,192,128]{2,1,0:T(8,128)(2,1)S(1)}, u32[]{:S(2)}, u32[]{:S(2)}) %collective-permute-start.4) | collective-permute-done | bytes 196640 | tf_op jit(solution)/shard_map/ppermute | solution.py:242
  130.4 0.9 collective-permute-done.5
  131.4 1.1 add_convert_fusion
  132.5 9.0 %all_to_all.23 = bf16[4,192,128]{2,1,0:T(8,128)(2,1)S(1)} all-to-all(bf16[4,192,128]{2,1,0:T(8,128)(2,1)S(1)} %add_convert_fusion), channel_id=1, replica_groups=mesh['yh'=2,'z'=8,'c'=2,'yl'=2,'x'=4] {'yh','c'}, dimensions={0} | all-to-all | bytes 393216 | tf_op jit(solution)/shard_map/all_to_all | solution.py:244
  141.5 0.9 copy.16
  (9 shorter events, 0.2 us)
Async XLA Ops:
  15.7 22.8 %copy-start = (bf16[4,240,128]{2,1,0:T(8,128)(2,1)}, bf16[4,240,128]{2,1,0:T(8,128)(2,1)S(1)}, u32[]{:S(2)}) copy-start(bf16[4,240,128]{2,1,0:T(8,128)(2,1)S(1)} %all_to_all.20.g0) | copy-start | bytes 737284
  15.7 12.9 %collective-permute-start.2 = (bf16[4,240,128]{2,1,0:T(8,128)(2,1)S(1)}, bf16[4,240,128]{2,1,0:T(8,128)(2,1)S(1)}, u32[]{:S(2)}, u32[]{:S(2)}) collective-permute-start(bf16[4,240,128]{2,1,0:T(8,128)(2,1)S(1)} %all_to_all.20.g0), channel_id=1, source_target_pairs={{96,0},{112,16},{0,32},{16,48},{32,64},{48,80},{64,96},{80,112},{9... | collective-permute-start | bytes 737288 | tf_op jit(solution)/shard_map/ppermute | solution.py:199
  18.7 15.4 %collective-permute-start.1 = (bf16[4,240,128]{2,1,0:T(8,128)(2,1)S(1)}, bf16[4,240,128]{2,1,0:T(8,128)(2,1)S(1)}, u32[]{:S(2)}, u32[]{:S(2)}) collective-permute-start(bf16[4,240,128]{2,1,0:T(8,128)(2,1)S(1)} %all_to_all.20.g0), channel_id=1, source_target_pairs={{32,0},{48,16},{64,32},{80,48},{96,64},{112,80},{0,96},{16,112},{3... | collective-permute-start | bytes 737288 | tf_op jit(solution)/shard_map/ppermute | solution.py:199
  21.8 16.8 %collective-permute-start = (bf16[4,240,128]{2,1,0:T(8,128)(2,1)S(1)}, bf16[4,240,128]{2,1,0:T(8,128)(2,1)S(1)}, u32[]{:S(2)}, u32[]{:S(2)}) collective-permute-start(bf16[4,240,128]{2,1,0:T(8,128)(2,1)S(1)} %all_to_all.20.g0), channel_id=1, source_target_pairs={{16,0},{32,16},{48,32},{64,48},{80,64},{96,80},{112,96},{0,112},{1... | collective-permute-start | bytes 737288 | tf_op jit(solution)/shard_map/ppermute | solution.py:199
  28.7 9.9 %copy-start.1 = (bf16[4,240,128]{2,1,0:T(8,128)(2,1)}, bf16[4,240,128]{2,1,0:T(8,128)(2,1)S(1)}, u32[]{:S(2)}) copy-start(bf16[4,240,128]{2,1,0:T(8,128)(2,1)S(1)} %collective-permute-done.2.g3) | copy-start | bytes 737284
  34.1 4.5 %copy-start.2 = (bf16[4,240,128]{2,1,0:T(8,128)(2,1)}, bf16[4,240,128]{2,1,0:T(8,128)(2,1)S(1)}, u32[]{:S(2)}) copy-start(bf16[4,240,128]{2,1,0:T(8,128)(2,1)S(1)} %collective-permute-done.1.g2) | copy-start | bytes 737284
  38.6 0.7 copy-start.3
  115.0 7.9 %collective-permute-start.3 = (bf16[4,192,128]{2,1,0:T(8,128)(2,1)}, bf16[4,192,128]{2,1,0:T(8,128)(2,1)S(1)}, u32[]{:S(2)}, u32[]{:S(2)}) collective-permute-start(bf16[4,192,128]{2,1,0:T(8,128)(2,1)} %get-tuple-element.14), channel_id=1, source_target_pairs={{0,16},{16,32},{32,48},{48,64},{64,80},{80,96},{96,112},{112,0},{1... | collective-permute-start | bytes 589832 | tf_op jit(solution)/shard_map/ppermute | solution.py:242
  115.8 14.7 %collective-permute-start.4 = (bf16[4,192,128]{2,1,0:T(8,128)(2,1)}, bf16[4,192,128]{2,1,0:T(8,128)(2,1)S(1)}, u32[]{:S(2)}, u32[]{:S(2)}) collective-permute-start(bf16[4,192,128]{2,1,0:T(8,128)(2,1)} %get-tuple-element.15), channel_id=1, source_target_pairs={{0,32},{16,48},{32,64},{48,80},{64,96},{80,112},{96,0},{112,16},{1... | collective-permute-start | bytes 589832 | tf_op jit(solution)/shard_map/ppermute | solution.py:242
  119.3 12.1 %collective-permute-start.5 = (bf16[4,192,128]{2,1,0:T(8,128)(2,1)}, bf16[4,192,128]{2,1,0:T(8,128)(2,1)S(1)}, u32[]{:S(2)}, u32[]{:S(2)}) collective-permute-start(bf16[4,192,128]{2,1,0:T(8,128)(2,1)} %get-tuple-element.16), channel_id=1, source_target_pairs={{0,96},{16,112},{32,0},{48,16},{64,32},{80,48},{96,64},{112,80},{1... | collective-permute-start | bytes 589832 | tf_op jit(solution)/shard_map/ppermute | solution.py:242

commit v2 on v1

v2 whole, which is shorter than its diff:
```python
import math

import jax
import jax.numpy as jnp
import numpy as np
from jax import lax
from jax.experimental import pallas as pl
from jax.experimental.pallas import tpu as pltpu
from jax.sharding import Mesh
from jax.sharding import PartitionSpec as P

BF = jnp.bfloat16
F32 = jnp.float32
CHIPS = 16
CHIP = ("yh", "z")
ROW = ("c", "yl", "x")
PEERS = 16
HALO = (0, 1, 2, 8, 13)
PLACES = ((0, 0), (1, 0), (2, 0), (0, 4), (1, 4), (2, 4), (3, 2), (3, 1), (3, 0))
STEPS = 17
SLOTS = 96
KROWS = 24
NONE = 1024
WIDE = 4 * SLOTS
TILES = 3 * len(PLACES)
ROWS = 384


def operator_parts(freq_total):
    lags = 2 * freq_total
    share = freq_total // PEERS
    order = np.array([(s % 8) * 2 * share + (s // 8) * share + f for s in range(PEERS) for f in range(share)])
    k = np.arange(-freq_total, 2 * freq_total)
    sines = np.where(k == 0, 0.0, -1.5 / np.tan(np.pi * np.where(k == 0, 1, k) / lags))
    f = order[:, None]
    h = order[None, :]
    couple = -(sines[h + f + freq_total] + sines[h - f + freq_total]) / lags
    top = lags + 1.5 * (lags - 1)
    real = np.where(order == 0, 2 * top + 3.0, top - 1.5 + 3.0) / lags
    imag = np.where(order == 0, 0.0, top + 1.5) / lags
    return couple, real, imag


def lists_of(gap):
    return ((0, 2 * gap - 1), (0, 2 * gap), (1, 2 * gap), (1, 2 * gap + 1))


def one_hot(index_ref, gap, side):
    rows = lax.broadcasted_iota(jnp.int32, (256, 128), 0)
    at = (gap * 2 + side) * 3
    picks = [(rows == index_ref[at + a : at + a + 1, :]).astype(F32).astype(BF) for a in range(3)]
    return jnp.concatenate(picks, 1)


def chip_rows(group):
    return jnp.concatenate([group[0, 0:ROWS, :], group[1, 0:ROWS, :]], 1)


def planes(x):
    return [(x[128 * c : 128 * c + 64], x[128 * c + 64 : 128 * c + 128]) for c in range(3)]


def cross_body(g0, g1, g2, g3, g4, out_ref, index_ref, lists):
    groups = (g0, g1, g2, g3, g4)
    lane = lax.broadcasted_iota(jnp.int32, (1, 128), 1)
    for i, g in enumerate(groups):
        for c in range(2):
            lists[i, c] = g[c, ROWS : ROWS + 2 * KROWS, :].astype(F32).astype(jnp.int32)
    for gap, (i, j) in enumerate(PLACES):
        for side, offsets in enumerate(((0, 0, 128, 128), (128, 0, 128, 0))):
            rolled = []
            for q, (c, k) in enumerate(lists_of(gap)):
                if 0 <= k < STEPS:
                    row = lists[i, c, KROWS * side + k : KROWS * side + k + 1, :] + offsets[q]
                    rolled.append(row if q == 0 else pltpu.roll(row, 128 - 32 * q, 1))
                else:
                    rolled.append(jnp.full((1, 128), NONE, jnp.int32))
            for a in range(3):
                at = (gap * 2 + side) * 3 + a
                index_ref[at : at + 1, :] = jnp.where(lane < 96 - 32 * a, rolled[a], rolled[a + 1])
    for gap, (i, j) in enumerate(PLACES):
        u = jnp.dot(chip_rows(groups[i]), one_hot(index_ref, gap, 0), preferred_element_type=F32)
        v = jnp.dot(chip_rows(groups[j]), one_hot(index_ref, gap, 1), preferred_element_type=F32)
        real = jnp.zeros((64, WIDE), F32)
        imag = jnp.zeros((64, WIDE), F32)
        for (ur, ui), (vr, vi) in zip(planes(u), planes(v)):
            real += ur * vr + ui * vi
            imag += ui * vr - ur * vi
        part = jnp.concatenate([real, imag], 0).astype(BF)
        for a in range(3):
            tile = 3 * gap + a
            half = tile % 2 * 128
            out_ref[tile // 2, :, half : half + 128] = part[:, 128 * a : 128 * a + 128]
    for tile in range(TILES, 2 * PEERS):
        half = tile % 2 * 128
        out_ref[tile // 2, :, half : half + 128] = jnp.zeros((128, 128), BF)


def spectral_body(cross_ref, couple_ref, couple_t_ref, diag_ref, out_ref):
    cross = cross_ref[...]
    size = couple_ref.shape[0]
    lags = 2.0 * size
    c0 = cross[:, 0:64, :].reshape(size, 256)
    c1 = cross[:, 64:128, :].reshape(size, 256)
    f0 = c0.astype(F32)
    f1 = c1.astype(F32)
    y0 = jnp.dot(couple_ref[...], c1, preferred_element_type=F32)
    y0 += diag_ref[:, 0:1] * f0 + (-3.0 / lags) * jnp.sum(f0, axis=0, keepdims=True)
    y1 = jnp.dot(couple_t_ref[...], c0, preferred_element_type=F32) + diag_ref[:, 1:2] * f1
    energy = jnp.sum(y0 * f0 + y1 * f1, axis=0, keepdims=True) / lags
    scale = 1.0 / jnp.sqrt(energy + 1e-5)
    out_ref[:, 0:64, :] = (y0 * scale).astype(BF).reshape(PEERS, 64, 256)
    out_ref[:, 64:128, :] = (y1 * scale).astype(BF).reshape(PEERS, 64, 256)


ORDER = (3, 4, 5, 6, 7, 8, 2, 1, 0)


def sums_body(index_ref, g0, g1, g2, g3, g4, spec_ref, o0, o1, o2, o3, o4, acc):
    groups = (g0, g1, g2, g3, g4)
    dims = (((1,), (1,)), ((), ()))
    begun = set()

    def add(place, value):
        acc[place] = acc[place] + value if place in begun else value
        begun.add(place)

    for gap in ORDER:
        i, j = PLACES[gap]
        pick_u = one_hot(index_ref, gap, 0)
        pick_v = one_hot(index_ref, gap, 1)
        u = jnp.dot(chip_rows(groups[i]), pick_u, preferred_element_type=F32)
        v = jnp.dot(chip_rows(groups[j]), pick_v, preferred_element_type=F32)
        tiles = [3 * gap + a for a in range(3)]
        spec = [spec_ref[t // 2, :, t % 2 * 128 : t % 2 * 128 + 128].astype(F32) for t in tiles]
        spec = jnp.concatenate(spec, 1)
        a0 = spec[0:64]
        a1 = spec[64:128]
        near = []
        far = []
        for (ur, ui), (vr, vi) in zip(planes(u), planes(v)):
            near += [(a0 * vr - a1 * vi).astype(BF), (a0 * vi + a1 * vr).astype(BF)]
            far += [(a0 * ur + a1 * ui).astype(BF), (a0 * ui - a1 * ur).astype(BF)]
        near = jnp.concatenate(near, 0)
        far = jnp.concatenate(far, 0)
        add(i, lax.dot_general(near, pick_u, dims, preferred_element_type=F32))
        add(j, lax.dot_general(far, pick_v, dims, preferred_element_type=F32))
    for i, o in enumerate((o0, o1, o2, o3, o4)):
        for c in range(2):
            o[c] = acc[i, :, 128 * c : 128 * c + 128].astype(o.dtype)


def whiten(spectra, band, first_freq):
    values = spectra.astype(F32).transpose(1, 2, 3, 0)
    meansq = jnp.mean(values * values, axis=(0, 1))
    freq = (first_freq + jnp.arange(values.shape[2], dtype=jnp.int32))[:, None]
    inside = (freq >= band[None, :, 0]) & (freq < band[None, :, 1])
    factor = jnp.where(inside, 1.0 / jnp.sqrt(jnp.maximum(meansq, 0.25)), 0.0)
    return (values * factor).astype(BF)


def on_device(spectra, band, pair_lists, pair_counts):
    stations, comps, parts, bins = spectra.shape
    freq_total = bins * 8
    params = pltpu.CompilerParams(vmem_limit_bytes=24 << 20)
    vmem = pl.BlockSpec(memory_space=pltpu.VMEM)
    lane = lax.axis_index(("yl", "x"))

    white = whiten(spectra, band, lane * bins)
    white = white.reshape(comps * parts, 2, bins // 2, stations).transpose(1, 0, 2, 3)
    white = white.reshape(2, ROWS, stations)
    used = jnp.arange(SLOTS, dtype=jnp.int32)[None, None, :] < pair_counts[0][:, None, None]
    lists = jnp.where(used, pair_lists[0].transpose(0, 2, 1), NONE).astype(BF)
    lists = jnp.pad(lists, ((0, KROWS - STEPS), (0, 0), (0, 128 - SLOTS)), constant_values=NONE)
    lists = lists.transpose(1, 0, 2).reshape(1, 2 * KROWS, 128)
    block = jnp.concatenate([white, jnp.broadcast_to(lists, (2, 2 * KROWS, 128))], 1)
    own = lax.all_to_all(block, "c", 0, 0, tiled=True)
    groups = [own]
    for d in HALO[1:]:
        groups.append(lax.ppermute(own, CHIP, [((w + d) % CHIPS, w) for w in range(CHIPS)]))

    pairs = jax.ShapeDtypeStruct((PEERS, 128, 256), BF)
    cross, index = pl.pallas_call(
        cross_body,
        in_specs=[vmem] * 5,
        out_specs=[vmem, vmem],
        out_shape=[pairs, jax.ShapeDtypeStruct((56, 128), jnp.int32)],
        scratch_shapes=[pltpu.VMEM((5, 2, 2 * KROWS, 128), jnp.int32)],
        compiler_params=params,
        name="cross",
    )(*groups)
    cross = lax.all_to_all(cross, ROW, 0, 0, tiled=True)

    couple, real, imag = operator_parts(freq_total)
    spectral = pl.pallas_call(
        spectral_body,
        in_specs=[vmem] * 4,
        out_specs=vmem,
        out_shape=pairs,
        compiler_params=params,
        name="spectral",
    )(
        cross,
        jnp.asarray(couple.astype(np.float32)).astype(BF),
        jnp.asarray(couple.T.astype(np.float32)).astype(BF),
        jnp.asarray(np.stack([real, imag], 1).astype(np.float32)),
    )
    spectral = lax.all_to_all(spectral, ROW, 0, 0, tiled=True)

    sums = pl.pallas_call(
        sums_body,
        in_specs=[vmem] * 7,
        out_specs=[vmem] * 5,
        out_shape=[jax.ShapeDtypeStruct((2, ROWS, 128), F32)] + [jax.ShapeDtypeStruct((2, ROWS, 128), BF)] * 4,
        scratch_shapes=[pltpu.VMEM((5, ROWS, 256), F32)],
        compiler_params=params,
        name="sums",
    )(index, *groups, spectral)
    total = sums[0]
    for d, part in zip(HALO[1:], sums[1:]):
        back = lax.ppermute(part, CHIP, [(w, (w + d) % CHIPS) for w in range(CHIPS)])
        total = total + back.astype(F32)
    total = lax.all_to_all(total.astype(BF), "c", 0, 0, tiled=True)
    total = total.reshape(2, comps, parts, bins // 2, stations).transpose(4, 1, 2, 0, 3)
    return total.reshape(stations, comps, parts, bins).astype(F32) / math.sqrt(SLOTS)


def solution(mesh):
    fine = Mesh(mesh.devices.reshape(2, 8, 2, 2, 4), ("yh", "z", "c", "yl", "x"))
    blk = ("yh", "z", "c")
    lag = ("yl", "x")
    in_specs = (P(blk, None, None, lag), P(blk, None), P(blk, None, None, None), P(blk, None))
    return jax.shard_map(
        on_device, mesh=fine, in_specs=in_specs, out_specs=P(blk, None, None, lag), check_vma=False
    )
```

time: 143 us -> 111 us (0.78)
  Pallas kernels: 30.5 us -> 8.65 us
  blocking collectives: 66.3 us -> 54.1 us
  starting transfers between devices: 12.3 us -> 17.9 us
  waiting for transfers between devices: 26.9 us -> 25.4 us
    pallas_call x2, Pallas kernels: 25.2 us -> 6.96 us  [the longest x1 4.42 us: on_device(): pl.pallas_call(sums_body, in_specs=[vmem] * 7, out_specs=[vmem] * 5, out_...]
    all_to_all x4, blocking collectives: 66.3 us -> 54.1 us  [the longest x1 21.9 us: on_device(): cross = lax.all_to_all(cross, ROW, 0, 0, tiled=True)]
    ppermute x6 -> x8, starting transfers between devices: 12.3 us -> 17.9 us  [the longest x4 8.98 us: on_device(): lax.ppermute(part, CHIP, [(w, (w + d) % CHIPS) for w in range(CHIPS)])]
    pallas_call x1, Pallas kernels: 5.31 us -> 1.7 us  [on_device(): pl.pallas_call(spectral_body, in_specs=[vmem] * 4, out_specs=vmem, out_sh...]
    ppermute x6 -> x8, waiting for transfers between devices: 26.9 us -> 25.4 us  [the longest x4 14.3 us: on_device(): lax.ppermute(own, CHIP, [((w + d) % CHIPS, w) for w in range(CHIPS)])]
  transfers between devices with their start and end apart: 6 -> 8, of which waited for: 6 -> 4; matrix products, arithmetic and copies ran while one was open for 0% -> 0% of each run, Pallas kernels for 0% -> 0%
where the time goes in v2:
time: 111 us
  blocking collectives  54.1 us (49%)
  waiting for transfers between devices  25.4 us (23%)
  starting transfers between devices  17.9 us (16%)
  Pallas kernels  8.65 us (8%)
  local copies, waits for them, and re-layouts  2.86 us (3%)
  other arithmetic  1.97 us (2%)
    all_to_all x1, blocking collectives, on_device(): cross = lax.all_to_all(cross, ROW, 0, 0, tiled=True)  21.9 us
    all_to_all x1, blocking collectives, on_device(): spectral = lax.all_to_all(spectral, ROW, 0, 0, tiled=True)  19.2 us
    ppermute x4, waiting for transfers between devices, on_device(): lax.ppermute(own, CHIP, [((w + d) % CHIPS, w) for w in range(CHIPS)])  14.3 us
    ppermute x4, waiting for transfers between devices, on_device(): lax.ppermute(part, CHIP, [(w, (w + d) % CHIPS) for w in range(CHIPS)])  11 us
    ppermute x4, starting transfers between devices, on_device(): lax.ppermute(part, CHIP, [(w, (w + d) % CHIPS) for w in range(CHIPS)])  8.98 us
    ppermute x4, starting transfers between devices, on_device(): lax.ppermute(own, CHIP, [((w + d) % CHIPS, w) for w in range(CHIPS)])  8.97 us
    all_to_all x1, blocking collectives, on_device(): own = lax.all_to_all(block, 'c', 0, 0, tiled=True)  6.9 us
    all_to_all x1, blocking collectives, on_device(): total = lax.all_to_all(total.astype(BF), 'c', 0, 0, tiled=True)  6.07 us
  transfers between devices with their start and end apart: 8, of which 4 were waited for; matrix products, arithmetic and copies ran while one was open for 0% of the time, Pallas kernels for 0%

profile of v2, /device:TPU:1, one launch (start us, length us, event | category | flops | bytes accessed | tf_op | source)
XLA Modules:
  0.0 111.0 jit_solution(4553926442782657867)
XLA Ops:
  0.0 0.8 slice_bitcast_fusion.1
  0.8 0.7 iota_compare_fusion
  1.5 1.1 copy.10
  2.6 0.1 rsqrt_select_fusion
  2.7 0.0 copy-start.2
  2.8 0.0 copy-start.1
  2.8 0.0 copy-start
  2.8 0.9 fusion.3
  3.8 6.9 %all_to_all.20.g0 = bf16[2,432,128]{2,1,0:T(8,128)(2,1)S(1)} all-to-all(bf16[2,432,128]{2,1,0:T(8,128)(2,1)S(1)} %pad_maximum_fusion), channel_id=1, replica_groups=mesh['yh'=2,'z'=8,'c'=2,'yl'=2,'x'=4] {'c'}, dimensions={0} | all-to-all | bytes 442368 | tf_op jit(solution)/shard_map/all_to_all | solution.py:177
  10.7 2.6 %collective-permute-start.3 = (bf16[2,432,128]{2,1,0:T(8,128)(2,1)S(1)}, bf16[2,432,128]{2,1,0:T(8,128)(2,1)S(1)}, u32[]{:S(2)}, u32[]{:S(2)}) collective-permute-start(bf16[2,432,128]{2,1,0:T(8,128)(2,1)S(1)} %all_to_all.20.g0), channel_id=1, source_target_pairs={{208,0},{224,16},{240,32},{0,48},{16,64},{32,80},{48,96},{64,112},... | collective-permute-start | bytes 663560 | tf_op jit(solution)/shard_map/ppermute | solution.py:180
  13.3 2.9 %collective-permute-start.2 = (bf16[2,432,128]{2,1,0:T(8,128)(2,1)S(1)}, bf16[2,432,128]{2,1,0:T(8,128)(2,1)S(1)}, u32[]{:S(2)}, u32[]{:S(2)}) collective-permute-start(bf16[2,432,128]{2,1,0:T(8,128)(2,1)S(1)} %all_to_all.20.g0), channel_id=1, source_target_pairs={{128,0},{144,16},{160,32},{176,48},{192,64},{208,80},{224,96},{240... | collective-permute-start | bytes 663560 | tf_op jit(solution)/shard_map/ppermute | solution.py:180
  16.2 3.0 %collective-permute-start.1 = (bf16[2,432,128]{2,1,0:T(8,128)(2,1)S(1)}, bf16[2,432,128]{2,1,0:T(8,128)(2,1)S(1)}, u32[]{:S(2)}, u32[]{:S(2)}) collective-permute-start(bf16[2,432,128]{2,1,0:T(8,128)(2,1)S(1)} %all_to_all.20.g0), channel_id=1, source_target_pairs={{32,0},{48,16},{64,32},{80,48},{96,64},{112,80},{128,96},{144,112}... | collective-permute-start | bytes 663560 | tf_op jit(solution)/shard_map/ppermute | solution.py:180
  19.2 0.5 collective-permute-start
  19.6 9.0 %collective-permute-done.3.g4 = bf16[2,432,128]{2,1,0:T(8,128)(2,1)S(1)} collective-permute-done((bf16[2,432,128]{2,1,0:T(8,128)(2,1)S(1)}, bf16[2,432,128]{2,1,0:T(8,128)(2,1)S(1)}, u32[]{:S(2)}, u32[]{:S(2)}) %collective-permute-start.3) | collective-permute-done | bytes 221216 | tf_op jit(solution)/shard_map/ppermute | solution.py:180
  28.6 0.0 collective-permute-done.2.g3
  28.6 0.0 collective-permute-done.1.g2
  28.6 5.4 %collective-permute-done.g1 = bf16[2,432,128]{2,1,0:T(8,128)(2,1)S(1)} collective-permute-done((bf16[2,432,128]{2,1,0:T(8,128)(2,1)S(1)}, bf16[2,432,128]{2,1,0:T(8,128)(2,1)S(1)}, u32[]{:S(2)}, u32[]{:S(2)}) %collective-permute-start) | collective-permute-done | bytes 221216 | tf_op jit(solution)/shard_map/ppermute | solution.py:180
  34.0 2.5 %cross.1 = (bf16[16,128,256]{2,1,0:T(8,128)(2,1)S(1)}, s32[56,128]{1,0:T(8,128)S(1)}) custom-call(bf16[2,432,128]{2,1,0:T(8,128)(2,1)S(1)} %all_to_all.20.g0, bf16[2,432,128]{2,1,0:T(8,128)(2,1)S(1)} %collective-permute-done.g1, bf16[2,432,128]{2,1,0:T(8,128)(2,1)S(1)} %collective-permute-done.1.g2, bf16[2,432,128]{2,1,0:T(8,128)(2,1)S(1)} %collective-permute-done.2.g3, ...), custom_call_target="tpu_custom_call" | custom-call | tf_op jit(solution)/shard_map/cross/pallas_call | solution.py:183
  36.5 21.9 %all_to_all.21.cross_ref = bf16[16,128,256]{2,1,0:T(8,128)(2,1)S(1)} all-to-all(bf16[16,128,256]{2,1,0:T(8,128)(2,1)S(1)} %get-tuple-element.13), channel_id=1, replica_groups=mesh['yh'=2,'z'=8,'c'=2,'yl'=2,'x'=4] {'c','yl','x'}, dimensions={0} | all-to-all | bytes 2097152 | tf_op jit(solution)/shard_map/all_to_all | solution.py:192
  58.4 0.0 copy-done.2
  58.4 0.0 copy-done.1
  58.4 0.0 copy-done
  58.5 1.7 %spectral.1 = bf16[16,128,256]{2,1,0:T(8,128)(2,1)S(1)} custom-call(bf16[16,128,256]{2,1,0:T(8,128)(2,1)S(1)} %all_to_all.21.cross_ref, bf16[1024,1024]{1,0:T(8,128)(2,1)S(1)} %copy-done.1, bf16[1024,1024]{1,0:T(8,128)(2,1)S(1)} %copy-done, f32[1024,2]{1,0:T(8,128)S(1)} %copy-done.2), custom_call_target="tpu_custom_call" | custom-call | tf_op jit(solution)/shard_map/spectral/pallas_call | solution.py:195
  60.2 19.2 %all_to_all.22.spec_ref = bf16[16,128,256]{2,1,0:T(8,128)(2,1)S(1)} all-to-all(bf16[16,128,256]{2,1,0:T(8,128)(2,1)S(1)} %spectral.1), channel_id=1, replica_groups=mesh['yh'=2,'z'=8,'c'=2,'yl'=2,'x'=4] {'c','yl','x'}, dimensions={0} | all-to-all | bytes 2097152 | tf_op jit(solution)/shard_map/all_to_all | solution.py:208
  79.4 4.4 %sums.1 = (f32[2,384,128]{2,1,0:T(8,128)S(1)}, bf16[2,384,128]{2,1,0:T(8,128)(2,1)S(1)}, bf16[2,384,128]{2,1,0:T(8,128)(2,1)S(1)}, bf16[2,384,128]{2,1,0:T(8,128)(2,1)S(1)}, bf16[2,384,128]{2,1,0:T(8,128)(2,1)S(1)}) custom-call(s32[56,128]{1,0:T(8,128)S(1)} %get-tuple-element.12.index_ref, bf16[2,432,128]{2,1,0:T(8,128)(2,1)S(1)} %all_to_all.20.g0, ...), custom_call_target="tpu_custom_call" | custom-call | tf_op jit(solution)/shard_map/sums/pallas_call | solution.py:210
  83.8 0.5 collective-permute-start.4
  84.3 3.5 %collective-permute-start.5 = (bf16[2,384,128]{2,1,0:T(8,128)(2,1)S(1)}, bf16[2,384,128]{2,1,0:T(8,128)(2,1)S(1)}, u32[]{:S(2)}, u32[]{:S(2)}) collective-permute-start(bf16[2,384,128]{2,1,0:T(8,128)(2,1)S(1)} %get-tuple-element.16), channel_id=1, source_target_pairs={{0,32},{16,48},{32,64},{48,80},{64,96},{80,112},{96,128},{112,144}... | collective-permute-start | bytes 589832 | tf_op jit(solution)/shard_map/ppermute | solution.py:221
  87.8 1.6 %collective-permute-start.6 = (bf16[2,384,128]{2,1,0:T(8,128)(2,1)S(1)}, bf16[2,384,128]{2,1,0:T(8,128)(2,1)S(1)}, u32[]{:S(2)}, u32[]{:S(2)}) collective-permute-start(bf16[2,384,128]{2,1,0:T(8,128)(2,1)S(1)} %get-tuple-element.17), channel_id=1, source_target_pairs={{0,128},{16,144},{32,160},{48,176},{64,192},{80,208},{96,224},{112... | collective-permute-start | bytes 589832 | tf_op jit(solution)/shard_map/ppermute | solution.py:221
  89.4 3.4 %collective-permute-start.7 = (bf16[2,384,128]{2,1,0:T(8,128)(2,1)S(1)}, bf16[2,384,128]{2,1,0:T(8,128)(2,1)S(1)}, u32[]{:S(2)}, u32[]{:S(2)}) collective-permute-start(bf16[2,384,128]{2,1,0:T(8,128)(2,1)S(1)} %get-tuple-element.18), channel_id=1, source_target_pairs={{0,208},{16,224},{32,240},{48,0},{64,16},{80,32},{96,48},{112,64},... | collective-permute-start | bytes 589832 | tf_op jit(solution)/shard_map/ppermute | solution.py:221
  92.8 1.7 %collective-permute-done.4 = bf16[2,384,128]{2,1,0:T(8,128)(2,1)S(1)} collective-permute-done((bf16[2,384,128]{2,1,0:T(8,128)(2,1)S(1)}, bf16[2,384,128]{2,1,0:T(8,128)(2,1)S(1)}, u32[]{:S(2)}, u32[]{:S(2)}) %collective-permute-start.4) | collective-permute-done | bytes 196640 | tf_op jit(solution)/shard_map/ppermute | solution.py:221
  94.5 9.3 %collective-permute-done.5 = bf16[2,384,128]{2,1,0:T(8,128)(2,1)S(1)} collective-permute-done((bf16[2,384,128]{2,1,0:T(8,128)(2,1)S(1)}, bf16[2,384,128]{2,1,0:T(8,128)(2,1)S(1)}, u32[]{:S(2)}, u32[]{:S(2)}) %collective-permute-start.5) | collective-permute-done | bytes 196640 | tf_op jit(solution)/shard_map/ppermute | solution.py:221
  103.8 0.0 collective-permute-done.6
  103.8 0.0 collective-permute-done.7
  103.8 0.1 add_convert_fusion
  104.0 6.1 %all_to_all.23 = bf16[2,384,128]{2,1,0:T(8,128)(2,1)S(1)} all-to-all(bf16[2,384,128]{2,1,0:T(8,128)(2,1)S(1)} %add_convert_fusion), channel_id=1, replica_groups=mesh['yh'=2,'z'=8,'c'=2,'yl'=2,'x'=4] {'c'}, dimensions={0} | all-to-all | bytes 393216 | tf_op jit(solution)/shard_map/all_to_all | solution.py:223
  110.1 0.9 copy.14
  (9 shorter events, 0.2 us)
Async XLA Ops:
  2.7 55.7 %copy-start.2 = (f32[1024,2]{1,0:T(8,128)S(1)}, f32[1024,2]{1,0:T(8,128)}, u32[]{:S(2)}) copy-start(f32[1024,2]{1,0:T(8,128)} %constant.36.clone.diag_ref) | copy-start | bytes 24580
  2.8 55.6 %copy-start.1 = (bf16[1024,1024]{1,0:T(8,128)(2,1)S(1)}, bf16[1024,1024]{1,0:T(8,128)(2,1)}, u32[]{:S(2)}) copy-start(bf16[1024,1024]{1,0:T(8,128)(2,1)} %constant.41.couple_ref) | copy-start | bytes 6291460
  2.8 55.6 %copy-start = (bf16[1024,1024]{1,0:T(8,128)(2,1)S(1)}, bf16[1024,1024]{1,0:T(8,128)(2,1)}, u32[]{:S(2)}) copy-start(bf16[1024,1024]{1,0:T(8,128)(2,1)} %constant.42.couple_t_ref) | copy-start | bytes 6291460
  10.7 18.0 %collective-permute-start.3 = (bf16[2,432,128]{2,1,0:T(8,128)(2,1)S(1)}, bf16[2,432,128]{2,1,0:T(8,128)(2,1)S(1)}, u32[]{:S(2)}, u32[]{:S(2)}) collective-permute-start(bf16[2,432,128]{2,1,0:T(8,128)(2,1)S(1)} %all_to_all.20.g0), channel_id=1, source_target_pairs={{208,0},{224,16},{240,32},{0,48},{16,64},{32,80},{48,96},{64,112},... | collective-permute-start | bytes 663560 | tf_op jit(solution)/shard_map/ppermute | solution.py:180
  13.3 15.3 %collective-permute-start.2 = (bf16[2,432,128]{2,1,0:T(8,128)(2,1)S(1)}, bf16[2,432,128]{2,1,0:T(8,128)(2,1)S(1)}, u32[]{:S(2)}, u32[]{:S(2)}) collective-permute-start(bf16[2,432,128]{2,1,0:T(8,128)(2,1)S(1)} %all_to_all.20.g0), channel_id=1, source_target_pairs={{128,0},{144,16},{160,32},{176,48},{192,64},{208,80},{224,96},{240... | collective-permute-start | bytes 663560 | tf_op jit(solution)/shard_map/ppermute | solution.py:180
  16.2 12.4 %collective-permute-start.1 = (bf16[2,432,128]{2,1,0:T(8,128)(2,1)S(1)}, bf16[2,432,128]{2,1,0:T(8,128)(2,1)S(1)}, u32[]{:S(2)}, u32[]{:S(2)}) collective-permute-start(bf16[2,432,128]{2,1,0:T(8,128)(2,1)S(1)} %all_to_all.20.g0), channel_id=1, source_target_pairs={{32,0},{48,16},{64,32},{80,48},{96,64},{112,80},{128,96},{144,112}... | collective-permute-start | bytes 663560 | tf_op jit(solution)/shard_map/ppermute | solution.py:180
  19.2 14.8 %collective-permute-start = (bf16[2,432,128]{2,1,0:T(8,128)(2,1)S(1)}, bf16[2,432,128]{2,1,0:T(8,128)(2,1)S(1)}, u32[]{:S(2)}, u32[]{:S(2)}) collective-permute-start(bf16[2,432,128]{2,1,0:T(8,128)(2,1)S(1)} %all_to_all.20.g0), channel_id=1, source_target_pairs={{16,0},{32,16},{48,32},{64,48},{80,64},{96,80},{112,96},{128,112},... | collective-permute-start | bytes 663560 | tf_op jit(solution)/shard_map/ppermute | solution.py:180
  83.8 10.7 %collective-permute-start.4 = (bf16[2,384,128]{2,1,0:T(8,128)(2,1)S(1)}, bf16[2,384,128]{2,1,0:T(8,128)(2,1)S(1)}, u32[]{:S(2)}, u32[]{:S(2)}) collective-permute-start(bf16[2,384,128]{2,1,0:T(8,128)(2,1)S(1)} %get-tuple-element.15), channel_id=1, source_target_pairs={{0,16},{16,32},{32,48},{48,64},{64,80},{80,96},{96,112},{112,128},... | collective-permute-start | bytes 589832 | tf_op jit(solution)/shard_map/ppermute | solution.py:221
  84.3 19.5 %collective-permute-start.5 = (bf16[2,384,128]{2,1,0:T(8,128)(2,1)S(1)}, bf16[2,384,128]{2,1,0:T(8,128)(2,1)S(1)}, u32[]{:S(2)}, u32[]{:S(2)}) collective-permute-start(bf16[2,384,128]{2,1,0:T(8,128)(2,1)S(1)} %get-tuple-element.16), channel_id=1, source_target_pairs={{0,32},{16,48},{32,64},{48,80},{64,96},{80,112},{96,128},{112,144}... | collective-permute-start | bytes 589832 | tf_op jit(solution)/shard_map/ppermute | solution.py:221
  87.8 16.0 %collective-permute-start.6 = (bf16[2,384,128]{2,1,0:T(8,128)(2,1)S(1)}, bf16[2,384,128]{2,1,0:T(8,128)(2,1)S(1)}, u32[]{:S(2)}, u32[]{:S(2)}) collective-permute-start(bf16[2,384,128]{2,1,0:T(8,128)(2,1)S(1)} %get-tuple-element.17), channel_id=1, source_target_pairs={{0,128},{16,144},{32,160},{48,176},{64,192},{80,208},{96,224},{112... | collective-permute-start | bytes 589832 | tf_op jit(solution)/shard_map/ppermute | solution.py:221
  89.4 14.4 %collective-permute-start.7 = (bf16[2,384,128]{2,1,0:T(8,128)(2,1)S(1)}, bf16[2,384,128]{2,1,0:T(8,128)(2,1)S(1)}, u32[]{:S(2)}, u32[]{:S(2)}) collective-permute-start(bf16[2,384,128]{2,1,0:T(8,128)(2,1)S(1)} %get-tuple-element.18), channel_id=1, source_target_pairs={{0,208},{16,224},{32,240},{48,0},{64,16},{80,32},{96,48},{112,64},... | collective-permute-start | bytes 589832 | tf_op jit(solution)/shard_map/ppermute | solution.py:221

commit v3 on v2

v3 whole, which is shorter than its diff:
```python
import math

import jax
import jax.numpy as jnp
import numpy as np
from jax import lax
from jax.experimental import pallas as pl
from jax.experimental.pallas import tpu as pltpu
from jax.sharding import Mesh
from jax.sharding import PartitionSpec as P

BF = jnp.bfloat16
F32 = jnp.float32
CHIPS = 16
CHIP = ("yh", "z")
ROW = ("c", "yl", "x")
PEERS = 16
HALO = (0, 1, 2, 8, 13)
PLACES = ((0, 0), (1, 0), (2, 0), (0, 4), (1, 4), (2, 4), (3, 2), (3, 1), (3, 0))
STEPS = 17
SLOTS = 96
FRONT = 16
TAIL = 32
NONE = 1024
WIDE = 4 * SLOTS
EARLY = (0, 1, 3, 4)
LATE = (2, 5, 6, 7, 8)
ALONE = tuple((gap, a) for gap in (2, 3, 4, 5, 6) for a in range(3)) + ((1, 0),)
SHARED = ((1, 1), (1, 2), (7, 0), (7, 1), (7, 2), (0, 0), (0, 1), (8, 0))
RESTS = {(8, 1): range(0, 8), (0, 2): range(8, 10), (8, 2): range(10, 12)}
LIST_ROWS = {6: 0, 7: 4, 8: 8, 1: 400, 4: 404, 2: 408, 5: 412, 0: 416, 3: 420}
SENT = {1: (16, 416), 2: (16, 416), 3: (0, 400), 4: (16, 416)}
CHUNK = 128 + 64 + 16
ROWS = 384


def operator_parts(freq_total):
    lags = 2 * freq_total
    share = freq_total // PEERS
    order = np.array([(s % 8) * 2 * share + (s // 8) * share + f for s in range(PEERS) for f in range(share)])
    k = np.arange(-freq_total, 2 * freq_total)
    sines = np.where(k == 0, 0.0, -1.5 / np.tan(np.pi * np.where(k == 0, 1, k) / lags))
    f = order[:, None]
    h = order[None, :]
    couple = -(sines[h + f + freq_total] + sines[h - f + freq_total]) / lags
    top = lags + 1.5 * (lags - 1)
    real = np.where(order == 0, 2 * top + 3.0, top - 1.5 + 3.0) / lags
    imag = np.where(order == 0, 0.0, top + 1.5) / lags
    return couple, real, imag


def lists_of(gap):
    four = ((0, 2 * gap - 1), (0, 2 * gap), (1, 2 * gap), (1, 2 * gap + 1))
    return sorted(four, key=lambda ck: not 0 <= ck[1] < STEPS)


def lanes(shape):
    return lax.broadcasted_iota(jnp.int32, shape, len(shape) - 1)


def turn(x, shift):
    shift %= 128
    return x if shift == 0 else pltpu.roll(x, shift, x.ndim - 1)


def fill_index(index_ref, groups, gaps):
    lane = lanes((1, 128))
    for n, gap in enumerate(gaps):
        row = LIST_ROWS[gap]
        lists = [groups[PLACES[gap][0]](c, row, row + 4).astype(F32).astype(jnp.int32) for c in range(2)]
        for side in range(2):
            rolled = []
            for q, (c, k) in enumerate(lists_of(gap)):
                block = c if side == 0 else (c - k) % 2
                at = 2 * (k - c - 2 * gap + 1) + side
                rolled.append(turn(lists[c][at : at + 1] + 128 * block, -32 * q))
            for a in range(3):
                at = (n * 2 + side) * 3 + a
                index_ref[at : at + 1, :] = jnp.where(lane < 96 - 32 * a, rolled[a], rolled[a + 1])


def one_hot(index_ref, n, side):
    rows = lax.broadcasted_iota(jnp.int32, (256, 128), 0)
    at = (n * 2 + side) * 3
    picks = [(rows == index_ref[at + a : at + a + 1, :]).astype(F32).astype(BF) for a in range(3)]
    return jnp.concatenate(picks, 1)


def both(group):
    return jnp.concatenate([group(0, FRONT, FRONT + ROWS), group(1, FRONT, FRONT + ROWS)], 1)


def by_block(ref, place):
    first = SENT[place][0] if place else 0
    return lambda block, lo, hi: ref[block, lo - first : hi - first, :]


def planes(x):
    return [(x[128 * c : 128 * c + 64], x[128 * c + 64 : 128 * c + 128]) for c in range(3)]


def cross_of(groups, index_ref, rows_ref, n, gap):
    i, j = PLACES[gap]
    u = jnp.dot(both(groups[i]), one_hot(index_ref, n, 0), preferred_element_type=F32)
    v = jnp.dot(both(groups[j]), one_hot(index_ref, n, 1), preferred_element_type=F32)
    rows_ref[n, 0] = u.astype(BF)
    rows_ref[n, 1] = v.astype(BF)
    real = jnp.zeros((64, WIDE), F32)
    imag = jnp.zeros((64, WIDE), F32)
    for (ur, ui), (vr, vi) in zip(planes(u), planes(v)):
        real += ur * vr + ui * vi
        imag += ui * vr - ur * vi
    return real, imag


def put_pairs(out_ref, gap, all_real, all_imag):
    lane = lanes((64, 128))
    slot = lanes((16, 128)) // 16
    for a in range(3):
        real = all_real[:, 128 * a : 128 * a + 128]
        imag = all_imag[:, 128 * a : 128 * a + 128]
        if (gap, a) in ALONE:
            peer = ALONE.index((gap, a))
            out_ref[peer, 0:64, :] = real.astype(BF)
            out_ref[peer, 64:128, :] = imag.astype(BF)
        elif (gap, a) in SHARED:
            peer = 2 * SHARED.index((gap, a))
            out_ref[peer, 128:192, :] = jnp.where(lane < 64, real, turn(imag, 64)).astype(BF)
            out_ref[peer + 1, 128:192, :] = jnp.where(lane < 64, turn(real, 64), imag).astype(BF)
        else:
            for m, peer in enumerate(RESTS[gap, a]):
                rest = jnp.zeros((16, 128), F32)
                for s in range(4):
                    rows = slice(16 * s, 16 * s + 16)
                    rest = jnp.where(slot == s, turn(real[rows], 16 * (s - m)), rest)
                    rest = jnp.where(slot == s + 4, turn(imag[rows], 16 * (s + 4 - m)), rest)
                out_ref[peer, 192:208, :] = rest.astype(BF)


def early_cross_body(g0, g1, g4, out_ref, index_ref, rows_ref):
    groups = {0: by_block(g0, 0), 1: by_block(g1, 1), 4: by_block(g4, 4)}
    fill_index(index_ref, groups, EARLY)
    for n, gap in enumerate(EARLY):
        put_pairs(out_ref, gap, *cross_of(groups, index_ref, rows_ref, n, gap))
    for peer in range(12, PEERS):
        out_ref[peer, 192:208, :] = jnp.zeros((16, 128), BF)


def late_cross_body(g0, g1, g2, g3, g4, begun, out_ref, index_ref, rows_ref):
    groups = [by_block(g, place) for place, g in enumerate((g0, g1, g2, g3, g4))]
    fill_index(index_ref, groups, LATE)
    for n, gap in enumerate(LATE):
        put_pairs(out_ref, gap, *cross_of(groups, index_ref, rows_ref, n, gap))


def spectral_body(cross_ref, couple_ref, couple_t_ref, diag_ref, out_ref):
    size = couple_ref.shape[0]
    lags = 2.0 * size
    lane = lanes((PEERS, 64, 128))
    slot = lanes((PEERS, 16, 128)) // 16
    half = cross_ref[:, 128:192, :].astype(F32)
    rest = cross_ref[:, 192:208, :].astype(F32)
    real_rest = jnp.concatenate([turn(rest, 64 - 16 * s) for s in range(4)], 1)
    imag_rest = jnp.concatenate([turn(rest, -16 * s) for s in range(4)], 1)
    real_half = jnp.where(lane < 64, half, real_rest).astype(BF)
    imag_half = jnp.where(lane < 64, turn(half, 64), imag_rest).astype(BF)
    c0 = jnp.concatenate([cross_ref[:, 0:64, :], real_half], 2).reshape(size, 256)
    c1 = jnp.concatenate([cross_ref[:, 64:128, :], imag_half], 2).reshape(size, 256)
    f0 = c0.astype(F32)
    f1 = c1.astype(F32)
    y0 = jnp.dot(couple_ref[...], c1, preferred_element_type=F32)
    y0 += diag_ref[:, 0:1] * f0 + (-3.0 / lags) * jnp.sum(f0, axis=0, keepdims=True)
    y1 = jnp.dot(couple_t_ref[...], c0, preferred_element_type=F32) + diag_ref[:, 1:2] * f1
    energy = jnp.sum(y0 * f0 + y1 * f1, axis=0, keepdims=True) / lags
    scale = 1.0 / jnp.sqrt(energy + 1e-5)
    a0 = (y0 * scale).reshape(PEERS, 64, 256)
    a1 = (y1 * scale).reshape(PEERS, 64, 256)
    out_ref[:, 0:64, :] = a0[:, :, 0:128].astype(BF)
    out_ref[:, 64:128, :] = a1[:, :, 0:128].astype(BF)
    a0 = a0[:, :, 128:256]
    a1 = a1[:, :, 128:256]
    out_ref[:, 128:192, :] = jnp.where(lane < 64, a0, turn(a1, 64)).astype(BF)
    rest = jnp.zeros((PEERS, 16, 128), F32)
    for s in range(4):
        rows = slice(16 * s, 16 * s + 16)
        rest = jnp.where(slot == s, turn(a0[:, rows], 16 * s - 64), rest)
        rest = jnp.where(slot == s + 4, turn(a1[:, rows], 16 * s), rest)
    out_ref[:, 192:208, :] = rest.astype(BF)


def spectra_of(spec_ref, gap, a):
    lane = lanes((64, 128))
    slot = lanes((16, 128)) // 16
    if (gap, a) in ALONE:
        peer = ALONE.index((gap, a))
        return spec_ref[peer, 0:64, :].astype(F32), spec_ref[peer, 64:128, :].astype(F32)
    if (gap, a) in SHARED:
        peer = 2 * SHARED.index((gap, a))
        left = spec_ref[peer, 128:192, :].astype(F32)
        right = spec_ref[peer + 1, 128:192, :].astype(F32)
        return jnp.where(lane < 64, left, turn(right, 64)), jnp.where(lane < 64, turn(left, 64), right)
    real = [jnp.zeros((16, 128), F32)] * 4
    imag = [jnp.zeros((16, 128), F32)] * 4
    for m, peer in enumerate(RESTS[gap, a]):
        rest = spec_ref[peer, 192:208, :].astype(F32)
        for s in range(4):
            real[s] = jnp.where(slot == m, turn(rest, 16 * (m - s)), real[s])
            imag[s] = jnp.where(slot == m, turn(rest, 16 * (m - s - 4)), imag[s])
    return jnp.concatenate(real, 0), jnp.concatenate(imag, 0)


def sums_of(rows_ref, index_ref, spec_ref, n, gap):
    i, j = PLACES[gap]
    dims = (((1,), (1,)), ((), ()))
    pick_u = one_hot(index_ref, n, 0)
    pick_v = one_hot(index_ref, n, 1)
    u = rows_ref[n, 0].astype(F32)
    v = rows_ref[n, 1].astype(F32)
    tiles = [spectra_of(spec_ref, gap, a) for a in range(3)]
    a0 = jnp.concatenate([t[0] for t in tiles], 1)
    a1 = jnp.concatenate([t[1] for t in tiles], 1)
    near = []
    far = []
    for (ur, ui), (vr, vi) in zip(planes(u), planes(v)):
        near += [(a0 * vr - a1 * vi).astype(BF), (a0 * vi + a1 * vr).astype(BF)]
        far += [(a0 * ur + a1 * ui).astype(BF), (a0 * ui - a1 * ur).astype(BF)]
    near = lax.dot_general(jnp.concatenate(near, 0), pick_u, dims, preferred_element_type=F32)
    far = lax.dot_general(jnp.concatenate(far, 0), pick_v, dims, preferred_element_type=F32)
    return (i, near), (j, far)


def sums_body(early_ref, early_rows, late_ref, late_rows, spec_ref, o0, o1, o2, o3, o4, acc):
    begun = set()
    for index_ref, rows_ref, gaps in ((late_ref, late_rows, LATE), (early_ref, early_rows, EARLY)):
        for n, gap in enumerate(gaps):
            for place, value in sums_of(rows_ref, index_ref, spec_ref, n, gap):
                acc[place] = acc[place] + value if place in begun else value
                begun.add(place)
    for place, o in enumerate((o0, o1, o2, o3, o4)):
        for c in range(2):
            o[c] = acc[place, :, 128 * c : 128 * c + 128].astype(o.dtype)


def block_body(at_ref, spectra_ref, tables_ref, out_ref):
    core, first_freq = at_ref[0], at_ref[1]
    band = tables_ref[STEPS]
    counts = tables_ref[STEPS + 1, 0:1, :]
    values = [[spectra_ref[c, r].astype(F32) for r in range(2)] for c in range(3)]
    power = jnp.zeros(values[0][0].shape, F32)
    for pair in values:
        power += pair[0] * pair[0] + pair[1] * pair[1]
    freq = first_freq + lax.broadcasted_iota(jnp.int32, power.shape, 0)
    inside = (freq >= band[0:1]) & (freq < band[1:2])
    factor = jnp.where(inside, 1.0 / jnp.sqrt(jnp.maximum(power / 6.0, 0.25)), 0.0)
    for c in range(3):
        for r in range(2):
            white = (values[c][r] * factor).astype(BF)
            row = FRONT + 128 * c + 64 * r
            for h in range(2):
                out_ref[h, row : row + 64, :] = white[64 * h : 64 * h + 64]
    lane = lanes((2, 128))
    unused = jnp.full((4, 128), NONE, jnp.int32)
    rows = {}
    for gap, row in LIST_ROWS.items():
        both_offsets = []
        for n in range(2):
            k = 2 * gap - 1 + n + core
            at = jnp.clip(k, 0, STEPS - 1)
            count = jnp.sum(jnp.where(lanes((1, 128)) == k, counts, 0), axis=1, keepdims=True)
            both_offsets.append(jnp.where(lane < count, tables_ref[at], NONE))
        rows[row] = jnp.concatenate(both_offsets, 0)
    front = jnp.concatenate([rows.get(4 * n, unused) for n in range(4)], 0)
    tail = jnp.concatenate([rows.get(FRONT + ROWS + 4 * n, unused) for n in range(8)], 0)
    for h in range(2):
        out_ref[h, 0:FRONT, :] = front.astype(F32).astype(BF)
        out_ref[h, FRONT + ROWS :, :] = tail.astype(F32).astype(BF)


def on_device(spectra, band, pair_lists, pair_counts):
    stations, comps, parts, bins = spectra.shape
    freq_total = bins * 8
    params = pltpu.CompilerParams(vmem_limit_bytes=24 << 20)
    vmem = pl.BlockSpec(memory_space=pltpu.VMEM)
    lane = lax.axis_index(("yl", "x"))

    def by_chip(x, shift):
        return lax.ppermute(x, CHIP, [((w + shift) % CHIPS, w) for w in range(CHIPS)])

    core = lax.axis_index("c")
    smem = pl.BlockSpec(memory_space=pltpu.SMEM)
    tables = jnp.concatenate(
        [
            jnp.pad(pair_lists[0].transpose(0, 2, 1), ((0, 0), (0, 0), (0, 128 - SLOTS))),
            band.T[None],
            jnp.pad(pair_counts[None], ((0, 0), (0, 1), (0, 128 - STEPS))),
        ],
        0,
    )
    block = pl.pallas_call(
        block_body,
        in_specs=[smem, vmem, vmem],
        out_specs=vmem,
        out_shape=jax.ShapeDtypeStruct((2, FRONT + ROWS + TAIL, stations), BF),
        compiler_params=params,
        name="block",
    )(
        jnp.stack([core, lane * bins]).astype(jnp.int32),
        spectra.transpose(1, 2, 3, 0),
        tables,
    )
    own = lax.all_to_all(block, "c", 0, 0, tiled=True)
    groups = [own]
    for place, (lo, hi) in SENT.items():
        groups.append(by_chip(own[:, lo:hi], HALO[place]))

    pairs = jax.ShapeDtypeStruct((PEERS, CHUNK, 128), BF)
    kept = [jax.ShapeDtypeStruct((n, 2, ROWS, WIDE), BF) for n in (len(EARLY), len(LATE))]
    cross, early, early_rows = pl.pallas_call(
        early_cross_body,
        in_specs=[vmem] * 3,
        out_specs=[vmem] * 3,
        out_shape=[pairs, jax.ShapeDtypeStruct((24, 128), jnp.int32), kept[0]],
        compiler_params=params,
        cost_estimate=pl.CostEstimate(flops=600000000, transcendentals=0, bytes_accessed=6291456),
        name="early_cross",
    )(groups[0], groups[1], groups[4])
    cross, late, late_rows = pl.pallas_call(
        late_cross_body,
        in_specs=[vmem] * 6,
        out_specs=[vmem] * 3,
        out_shape=[pairs, jax.ShapeDtypeStruct((32, 128), jnp.int32), kept[1]],
        input_output_aliases={5: 0},
        compiler_params=params,
        cost_estimate=pl.CostEstimate(flops=800000000, transcendentals=0, bytes_accessed=6291456),
        name="late_cross",
    )(*groups, cross)
    cross = lax.all_to_all(cross, ROW, 0, 0, tiled=True)

    couple, real, imag = operator_parts(freq_total)
    spectral = pl.pallas_call(
        spectral_body,
        in_specs=[vmem] * 4,
        out_specs=vmem,
        out_shape=pairs,
        compiler_params=params,
        cost_estimate=pl.CostEstimate(flops=1100000000, transcendentals=0, bytes_accessed=6291456),
        name="spectral",
    )(
        cross,
        jnp.asarray(couple.astype(np.float32)).astype(BF),
        jnp.asarray(couple.T.astype(np.float32)).astype(BF),
        jnp.asarray(np.stack([real, imag], 1).astype(np.float32)),
    )
    spectral = lax.all_to_all(spectral, ROW, 0, 0, tiled=True)

    chip = jax.ShapeDtypeStruct((2, ROWS, 128), BF)
    sums = pl.pallas_call(
        sums_body,
        in_specs=[vmem] * 5,
        out_specs=[vmem] * 5,
        out_shape=[jax.ShapeDtypeStruct((2, ROWS, 128), F32)] + [chip] * 4,
        scratch_shapes=[pltpu.VMEM((5, ROWS, 256), F32)],
        compiler_params=params,
        name="sums",
    )(early, early_rows, late, late_rows, spectral)
    total = sums[0]
    for place in (4, 1, 2, 3):
        total = total + by_chip(sums[place], -HALO[place]).astype(F32)
    total = lax.all_to_all(total.astype(BF), "c", 0, 0, tiled=True)
    total = total.reshape(2, comps, parts, bins // 2, stations).transpose(4, 1, 2, 0, 3)
    return total.reshape(stations, comps, parts, bins).astype(F32) / math.sqrt(SLOTS)


def solution(mesh):
    fine = Mesh(mesh.devices.reshape(2, 8, 2, 2, 4), ("yh", "z", "c", "yl", "x"))
    blk = ("yh", "z", "c")
    lag = ("yl", "x")
    in_specs = (P(blk, None, None, lag), P(blk, None), P(blk, None, None, None), P(blk, None))
    return jax.shard_map(
        on_device, mesh=fine, in_specs=in_specs, out_specs=P(blk, None, None, lag), check_vma=False
    )
```

time: 111 us -> 103 us (0.928)
  blocking collectives: 54.1 us -> 48.2 us
    all_to_all x1, blocking collectives: 19.2 us -> 17.1 us  [on_device(): spectral = lax.all_to_all(spectral, ROW, 0, 0, tiled=True)]
    all_to_all x1, blocking collectives: 6.07 us -> 4.03 us  [on_device(): total = lax.all_to_all(total.astype(BF), 'c', 0, 0, tiled=True)]
    all_to_all x1, blocking collectives: 21.9 us -> 20.3 us  [on_device(): cross = lax.all_to_all(cross, ROW, 0, 0, tiled=True)]
    pallas_call x2 -> x4, Pallas kernels: 6.96 us -> 6.53 us  [the longest x1 2.81 us: on_device(): pl.pallas_call(sums_body, in_specs=[vmem] * 5, out_specs=[vmem] * 5, out_...]
  transfers between devices with their start and end apart: 8 -> 8, of which waited for: 4 -> 5; matrix products, arithmetic and copies ran while one was open for 0% -> 0% of each run, Pallas kernels for 0% -> 1%
where the time goes in v3:
time: 103 us
  blocking collectives  48.2 us (47%)
  waiting for transfers between devices  25.4 us (25%)
  starting transfers between devices  17.8 us (17%)
  Pallas kernels  8.5 us (8%)
  local copies, waits for them, and re-layouts  2.11 us (2%)
    ppermute x8, waiting for transfers between devices, by_chip(): lax.ppermute(x, CHIP, [((w + shift) % CHIPS, w) for w in range(CHIPS)])  25.4 us
    all_to_all x1, blocking collectives, on_device(): cross = lax.all_to_all(cross, ROW, 0, 0, tiled=True)  20.3 us
    ppermute x8, starting transfers between devices, by_chip(): lax.ppermute(x, CHIP, [((w + shift) % CHIPS, w) for w in range(CHIPS)])  17.8 us
    all_to_all x1, blocking collectives, on_device(): spectral = lax.all_to_all(spectral, ROW, 0, 0, tiled=True)  17.1 us
    all_to_all x1, blocking collectives, on_device(): own = lax.all_to_all(block, 'c', 0, 0, tiled=True)  6.77 us
    all_to_all x1, blocking collectives, on_device(): total = lax.all_to_all(total.astype(BF), 'c', 0, 0, tiled=True)  4.03 us
    pallas_call x1, Pallas kernels, on_device(): pl.pallas_call(sums_body, in_specs=[vmem] * 5, out_specs=[vmem] * 5, out_...  2.81 us
  transfers between devices with their start and end apart: 8, of which 5 were waited for; matrix products, arithmetic and copies ran while one was open for 0% of the time, Pallas kernels for 1%

profile of v3, /device:TPU:1, one launch (start us, length us, event | category | flops | bytes accessed | tf_op | source)
XLA Modules:
  0.0 103.0 jit_solution(17908829420641856913)
XLA Ops:
  0.0 1.1 %copy.11 = bf16[128,3,2,128]{0,3,2,1:T(8,128)(2,1)S(1)} copy(bf16[128,3,2,128]{3,2,1,0:T(2,128)(2,1)} %param.7) | data formatting | bytes 393216 | tf_op args[0]
  1.1 0.1 pad_add_fusion.2.at_ref
  1.2 0.7 pad_add_fusion.tables_ref
  1.9 0.8 block.1
  2.7 6.8 %all_to_all.20.g0 = bf16[2,432,128]{2,1,0:T(8,128)(2,1)S(1)} all-to-all(bf16[2,432,128]{2,1,0:T(8,128)(2,1)S(1)} %block.1), channel_id=1, replica_groups=mesh['yh'=2,'z'=8,'c'=2,'yl'=2,'x'=4] {'c'}, dimensions={0} | all-to-all | bytes 442368 | tf_op jit(solution)/shard_map/all_to_all | solution.py:311
  9.5 0.1 fusion
  9.5 2.7 %collective-permute-start.1 = (bf16[2,400,128]{2,1,0:T(8,128)(2,1)S(1)}, bf16[2,400,128]{2,1,0:T(8,128)(2,1)S(1)}, u32[]{:S(2)}, u32[]{:S(2)}) collective-permute-start(bf16[2,400,128]{2,1,0:T(8,128)(2,1)S(1)} %get-tuple-element.28), channel_id=1, source_target_pairs={{208,0},{224,16},{240,32},{0,48},{16,64},{32,80},{48,96},{64,112},... | collective-permute-start | bytes 614408 | tf_op jit(solution)/shard_map/ppermute | solution.py:287
  12.2 4.0 %collective-permute-start = (bf16[2,400,128]{2,1,0:T(8,128)(2,1)S(1)}, bf16[2,400,128]{2,1,0:T(8,128)(2,1)S(1)}, u32[]{:S(2)}, u32[]{:S(2)}) collective-permute-start(bf16[2,400,128]{2,1,0:T(8,128)(2,1)S(1)} %get-tuple-element.28), channel_id=1, source_target_pairs={{16,0},{32,16},{48,32},{64,48},{80,64},{96,80},{112,96},{128,112},... | collective-permute-start | bytes 614408 | tf_op jit(solution)/shard_map/ppermute | solution.py:287
  16.2 2.4 %collective-permute-start.3 = (bf16[2,400,128]{2,1,0:T(8,128)(2,1)S(1)}, bf16[2,400,128]{2,1,0:T(8,128)(2,1)S(1)}, u32[]{:S(2)}, u32[]{:S(2)}) collective-permute-start(bf16[2,400,128]{2,1,0:T(8,128)(2,1)S(1)} %get-tuple-element.27), channel_id=1, source_target_pairs={{128,0},{144,16},{160,32},{176,48},{192,64},{208,80},{224,96},{240... | collective-permute-start | bytes 614408 | tf_op jit(solution)/shard_map/ppermute | solution.py:287
  18.6 0.0 collective-permute-start.2
  18.6 8.6 %collective-permute-done.1.g4 = bf16[2,400,128]{2,1,0:T(8,128)(2,1)S(1)} collective-permute-done((bf16[2,400,128]{2,1,0:T(8,128)(2,1)S(1)}, bf16[2,400,128]{2,1,0:T(8,128)(2,1)S(1)}, u32[]{:S(2)}, u32[]{:S(2)}) %collective-permute-start.1) | collective-permute-done | bytes 204832 | tf_op jit(solution)/shard_map/ppermute | solution.py:287
  27.2 0.0 collective-permute-done.g1
  27.2 0.0 copy-start.2
  27.2 1.3 %early_cross.1 = (bf16[16,208,128]{2,1,0:T(8,128)(2,1)S(1)}, s32[24,128]{1,0:T(8,128)S(1)}, bf16[4,2,384,384]{3,2,1,0:T(8,128)(2,1)S(1)}) custom-call(bf16[2,432,128]{2,1,0:T(8,128)(2,1)S(1)} %all_to_all.20.g0, bf16[2,400,128]{2,1,0:T(8,128)(2,1)S(1)} %collective-permute-done.g1, bf16[2,400,128]{2,1,0:T(8,128)(2,1)S(1)} %collective-permute-done.1.g4), custom_call_target="tpu_custom_call" | custom-call | flops 600000000 | bytes 6291456 | tf_op jit(solution)/shard_map/early_cross/pallas_call | solution.py:318
  28.5 0.0 copy-start
  28.5 0.0 copy-start.1
  28.5 0.0 collective-permute-done.3.g3
  28.5 1.5 %collective-permute-done.2.g2 = bf16[2,400,128]{2,1,0:T(8,128)(2,1)S(1)} collective-permute-done((bf16[2,400,128]{2,1,0:T(8,128)(2,1)S(1)}, bf16[2,400,128]{2,1,0:T(8,128)(2,1)S(1)}, u32[]{:S(2)}, u32[]{:S(2)}) %collective-permute-start.2) | collective-permute-done | bytes 204832 | tf_op jit(solution)/shard_map/ppermute | solution.py:287
  30.0 1.7 %late_cross.1 = (bf16[16,208,128]{2,1,0:T(8,128)(2,1)S(1)}, s32[32,128]{1,0:T(8,128)S(1)}, bf16[5,2,384,384]{3,2,1,0:T(8,128)(2,1)S(1)}) custom-call(bf16[2,432,128]{2,1,0:T(8,128)(2,1)S(1)} %all_to_all.20.g0, bf16[2,400,128]{2,1,0:T(8,128)(2,1)S(1)} %collective-permute-done.g1, ...), custom_call_target="tpu_custom_call", output_to_operand_aliasing={{0}: (5, {})} | custom-call | flops 800000000 | bytes 6291456 | tf_op jit(solution)/shard_map/late_cross/pallas_call | solution.py:327
  31.7 20.3 %all_to_all.21.cross_ref = bf16[16,208,128]{2,1,0:T(8,128)(2,1)S(1)} all-to-all(bf16[16,208,128]{2,1,0:T(8,128)(2,1)S(1)} %get-tuple-element.21), channel_id=1, replica_groups=mesh['yh'=2,'z'=8,'c'=2,'yl'=2,'x'=4] {'c','yl','x'}, dimensions={0} | all-to-all | bytes 1703936 | tf_op jit(solution)/shard_map/all_to_all | solution.py:337
  52.0 0.0 copy-done.2
  52.0 0.0 copy-done
  52.0 0.0 copy-done.1
  52.0 2.0 %spectral.1 = bf16[16,208,128]{2,1,0:T(8,128)(2,1)S(1)} custom-call(bf16[16,208,128]{2,1,0:T(8,128)(2,1)S(1)} %all_to_all.21.cross_ref, bf16[1024,1024]{1,0:T(8,128)(2,1)S(1)} %copy-done.1, bf16[1024,1024]{1,0:T(8,128)(2,1)S(1)} %copy-done, f32[1024,2]{1,0:T(8,128)S(1)} %copy-done.2), custom_call_target="tpu_custom_call" | custom-call | flops 1100000000 | bytes 6291456 | tf_op jit(solution)/shard_map/spectral/pallas_call | solution.py:340
  54.0 17.1 %all_to_all.22.spec_ref = bf16[16,208,128]{2,1,0:T(8,128)(2,1)S(1)} all-to-all(bf16[16,208,128]{2,1,0:T(8,128)(2,1)S(1)} %spectral.1), channel_id=1, replica_groups=mesh['yh'=2,'z'=8,'c'=2,'yl'=2,'x'=4] {'c','yl','x'}, dimensions={0} | all-to-all | bytes 1703936 | tf_op jit(solution)/shard_map/all_to_all | solution.py:354
  71.1 2.8 %sums.1 = (f32[2,384,128]{2,1,0:T(8,128)S(1)}, bf16[2,384,128]{2,1,0:T(8,128)(2,1)S(1)}, bf16[2,384,128]{2,1,0:T(8,128)(2,1)S(1)}, bf16[2,384,128]{2,1,0:T(8,128)(2,1)S(1)}, bf16[2,384,128]{2,1,0:T(8,128)(2,1)S(1)}) custom-call(s32[24,128]{1,0:T(8,128)S(1)} %get-tuple-element.16.early_ref, bf16[4,2,384,384]{3,2,1,0:T(8,128)(2,1)S(1)} %get-tuple-element.17.early_rows, ...), custom_call_target="tpu_custom_call" | custom-call | tf_op jit(solution)/shard_map/sums/pallas_call | solution.py:357
  73.9 5.1 %collective-permute-start.4 = (bf16[2,384,128]{2,1,0:T(8,128)(2,1)S(1)}, bf16[2,384,128]{2,1,0:T(8,128)(2,1)S(1)}, u32[]{:S(2)}, u32[]{:S(2)}) collective-permute-start(bf16[2,384,128]{2,1,0:T(8,128)(2,1)S(1)} %get-tuple-element.23), channel_id=1, source_target_pairs={{48,0},{64,16},{80,32},{96,48},{112,64},{128,80},{144,96},{160,112... | collective-permute-start | bytes 589832 | tf_op jit(solution)/shard_map/ppermute | solution.py:287
  79.0 2.2 %collective-permute-start.5 = (bf16[2,384,128]{2,1,0:T(8,128)(2,1)S(1)}, bf16[2,384,128]{2,1,0:T(8,128)(2,1)S(1)}, u32[]{:S(2)}, u32[]{:S(2)}) collective-permute-start(bf16[2,384,128]{2,1,0:T(8,128)(2,1)S(1)} %get-tuple-element.24), channel_id=1, source_target_pairs={{240,0},{0,16},{16,32},{32,48},{48,64},{64,80},{80,96},{96,112},{1... | collective-permute-start | bytes 589832 | tf_op jit(solution)/shard_map/ppermute | solution.py:287
  81.2 0.0 collective-permute-start.6
  81.2 1.4 %collective-permute-start.7 = (bf16[2,384,128]{2,1,0:T(8,128)(2,1)S(1)}, bf16[2,384,128]{2,1,0:T(8,128)(2,1)S(1)}, u32[]{:S(2)}, u32[]{:S(2)}) collective-permute-start(bf16[2,384,128]{2,1,0:T(8,128)(2,1)S(1)} %get-tuple-element.26), channel_id=1, source_target_pairs={{128,0},{144,16},{160,32},{176,48},{192,64},{208,80},{224,96},{240... | collective-permute-start | bytes 589832 | tf_op jit(solution)/shard_map/ppermute | solution.py:287
  82.6 8.8 %collective-permute-done.4 = bf16[2,384,128]{2,1,0:T(8,128)(2,1)S(1)} collective-permute-done((bf16[2,384,128]{2,1,0:T(8,128)(2,1)S(1)}, bf16[2,384,128]{2,1,0:T(8,128)(2,1)S(1)}, u32[]{:S(2)}, u32[]{:S(2)}) %collective-permute-start.4) | collective-permute-done | bytes 196640 | tf_op jit(solution)/shard_map/ppermute | solution.py:287
  91.4 0.0 collective-permute-done.5
  91.4 1.7 %collective-permute-done.6 = bf16[2,384,128]{2,1,0:T(8,128)(2,1)S(1)} collective-permute-done((bf16[2,384,128]{2,1,0:T(8,128)(2,1)S(1)}, bf16[2,384,128]{2,1,0:T(8,128)(2,1)S(1)}, u32[]{:S(2)}, u32[]{:S(2)}) %collective-permute-start.6) | collective-permute-done | bytes 196640 | tf_op jit(solution)/shard_map/ppermute | solution.py:287
  93.2 4.7 %collective-permute-done.7 = bf16[2,384,128]{2,1,0:T(8,128)(2,1)S(1)} collective-permute-done((bf16[2,384,128]{2,1,0:T(8,128)(2,1)S(1)}, bf16[2,384,128]{2,1,0:T(8,128)(2,1)S(1)}, u32[]{:S(2)}, u32[]{:S(2)}) %collective-permute-start.7) | collective-permute-done | bytes 196640 | tf_op jit(solution)/shard_map/ppermute | solution.py:287
  97.9 0.1 add_convert_fusion
  98.0 4.0 %all_to_all.23 = bf16[2,384,128]{2,1,0:T(8,128)(2,1)S(1)} all-to-all(bf16[2,384,128]{2,1,0:T(8,128)(2,1)S(1)} %add_convert_fusion), channel_id=1, replica_groups=mesh['yh'=2,'z'=8,'c'=2,'yl'=2,'x'=4] {'c'}, dimensions={0} | all-to-all | bytes 393216 | tf_op jit(solution)/shard_map/all_to_all | solution.py:369
  102.1 0.9 copy.13
  (2 shorter events, 0.1 us)
Async XLA Ops:
  9.5 17.7 %collective-permute-start.1 = (bf16[2,400,128]{2,1,0:T(8,128)(2,1)S(1)}, bf16[2,400,128]{2,1,0:T(8,128)(2,1)S(1)}, u32[]{:S(2)}, u32[]{:S(2)}) collective-permute-start(bf16[2,400,128]{2,1,0:T(8,128)(2,1)S(1)} %get-tuple-element.28), channel_id=1, source_target_pairs={{208,0},{224,16},{240,32},{0,48},{16,64},{32,80},{48,96},{64,112},... | collective-permute-start | bytes 614408 | tf_op jit(solution)/shard_map/ppermute | solution.py:287
  12.2 15.0 %collective-permute-start = (bf16[2,400,128]{2,1,0:T(8,128)(2,1)S(1)}, bf16[2,400,128]{2,1,0:T(8,128)(2,1)S(1)}, u32[]{:S(2)}, u32[]{:S(2)}) collective-permute-start(bf16[2,400,128]{2,1,0:T(8,128)(2,1)S(1)} %get-tuple-element.28), channel_id=1, source_target_pairs={{16,0},{32,16},{48,32},{64,48},{80,64},{96,80},{112,96},{128,112},... | collective-permute-start | bytes 614408 | tf_op jit(solution)/shard_map/ppermute | solution.py:287
  16.2 12.3 %collective-permute-start.3 = (bf16[2,400,128]{2,1,0:T(8,128)(2,1)S(1)}, bf16[2,400,128]{2,1,0:T(8,128)(2,1)S(1)}, u32[]{:S(2)}, u32[]{:S(2)}) collective-permute-start(bf16[2,400,128]{2,1,0:T(8,128)(2,1)S(1)} %get-tuple-element.27), channel_id=1, source_target_pairs={{128,0},{144,16},{160,32},{176,48},{192,64},{208,80},{224,96},{240... | collective-permute-start | bytes 614408 | tf_op jit(solution)/shard_map/ppermute | solution.py:287
  18.6 11.5 %collective-permute-start.2 = (bf16[2,400,128]{2,1,0:T(8,128)(2,1)S(1)}, bf16[2,400,128]{2,1,0:T(8,128)(2,1)S(1)}, u32[]{:S(2)}, u32[]{:S(2)}) collective-permute-start(bf16[2,400,128]{2,1,0:T(8,128)(2,1)S(1)} %get-tuple-element.28), channel_id=1, source_target_pairs={{32,0},{48,16},{64,32},{80,48},{96,64},{112,80},{128,96},{144,112}... | collective-permute-start | bytes 614408 | tf_op jit(solution)/shard_map/ppermute | solution.py:287
  27.2 24.8 %copy-start.2 = (f32[1024,2]{1,0:T(8,128)S(1)}, f32[1024,2]{1,0:T(8,128)}, u32[]{:S(2)}) copy-start(f32[1024,2]{1,0:T(8,128)} %constant.29.clone.diag_ref) | copy-start | bytes 24580
  28.5 23.6 %copy-start = (bf16[1024,1024]{1,0:T(8,128)(2,1)S(1)}, bf16[1024,1024]{1,0:T(8,128)(2,1)}, u32[]{:S(2)}) copy-start(bf16[1024,1024]{1,0:T(8,128)(2,1)} %constant.37.couple_t_ref) | copy-start | bytes 6291460
  28.5 23.5 %copy-start.1 = (bf16[1024,1024]{1,0:T(8,128)(2,1)S(1)}, bf16[1024,1024]{1,0:T(8,128)(2,1)}, u32[]{:S(2)}) copy-start(bf16[1024,1024]{1,0:T(8,128)(2,1)} %constant.36.couple_ref) | copy-start | bytes 6291460
  73.9 17.5 %collective-permute-start.4 = (bf16[2,384,128]{2,1,0:T(8,128)(2,1)S(1)}, bf16[2,384,128]{2,1,0:T(8,128)(2,1)S(1)}, u32[]{:S(2)}, u32[]{:S(2)}) collective-permute-start(bf16[2,384,128]{2,1,0:T(8,128)(2,1)S(1)} %get-tuple-element.23), channel_id=1, source_target_pairs={{48,0},{64,16},{80,32},{96,48},{112,64},{128,80},{144,96},{160,112... | collective-permute-start | bytes 589832 | tf_op jit(solution)/shard_map/ppermute | solution.py:287
  79.0 12.4 %collective-permute-start.5 = (bf16[2,384,128]{2,1,0:T(8,128)(2,1)S(1)}, bf16[2,384,128]{2,1,0:T(8,128)(2,1)S(1)}, u32[]{:S(2)}, u32[]{:S(2)}) collective-permute-start(bf16[2,384,128]{2,1,0:T(8,128)(2,1)S(1)} %get-tuple-element.24), channel_id=1, source_target_pairs={{240,0},{0,16},{16,32},{32,48},{48,64},{64,80},{80,96},{96,112},{1... | collective-permute-start | bytes 589832 | tf_op jit(solution)/shard_map/ppermute | solution.py:287
  81.2 11.9 %collective-permute-start.6 = (bf16[2,384,128]{2,1,0:T(8,128)(2,1)S(1)}, bf16[2,384,128]{2,1,0:T(8,128)(2,1)S(1)}, u32[]{:S(2)}, u32[]{:S(2)}) collective-permute-start(bf16[2,384,128]{2,1,0:T(8,128)(2,1)S(1)} %get-tuple-element.25), channel_id=1, source_target_pairs={{224,0},{240,16},{0,32},{16,48},{32,64},{48,80},{64,96},{80,112},{... | collective-permute-start | bytes 589832 | tf_op jit(solution)/shard_map/ppermute | solution.py:287
  81.2 16.6 %collective-permute-start.7 = (bf16[2,384,128]{2,1,0:T(8,128)(2,1)S(1)}, bf16[2,384,128]{2,1,0:T(8,128)(2,1)S(1)}, u32[]{:S(2)}, u32[]{:S(2)}) collective-permute-start(bf16[2,384,128]{2,1,0:T(8,128)(2,1)S(1)} %get-tuple-element.26), channel_id=1, source_target_pairs={{128,0},{144,16},{160,32},{176,48},{192,64},{208,80},{224,96},{240... | collective-permute-start | bytes 589832 | tf_op jit(solution)/shard_map/ppermute | solution.py:287

commit v4 on v3

--- a/solution.py
+++ b/solution.py
@@ -364,7 +364,7 @@
         name="sums",
     )(early, early_rows, late, late_rows, spectral)
     total = sums[0]
-    for place in (4, 1, 2, 3):
+    for place in (1, 2, 4, 3):
         total = total + by_chip(sums[place], -HALO[place]).astype(F32)
     total = lax.all_to_all(total.astype(BF), "c", 0, 0, tiled=True)
     total = total.reshape(2, comps, parts, bins // 2, stations).transpose(4, 1, 2, 0, 3)

time: 103 us -> 99.7 us (0.968)
  waiting for transfers between devices: 25.4 us -> 20.6 us
  starting transfers between devices: 17.8 us -> 18.9 us
    ppermute x8, waiting for transfers between devices: 25.4 us -> 20.6 us  [by_chip(): lax.ppermute(x, CHIP, [((w + shift) % CHIPS, w) for w in range(CHIPS)])]
    ppermute x8, starting transfers between devices: 17.8 us -> 18.9 us  [by_chip(): lax.ppermute(x, CHIP, [((w + shift) % CHIPS, w) for w in range(CHIPS)])]
where the time goes in v4:
time: 99.7 us; the launch traced here: 99.4 us
  blocking collectives  48.2 us (48%)
  waiting for transfers between devices  20.6 us (21%)
  starting transfers between devices  18.9 us (19%)
  Pallas kernels  8.5 us (9%)
  local copies, waits for them, and re-layouts  2.11 us (2%)
    ppermute x8, waiting for transfers between devices, by_chip(): lax.ppermute(x, CHIP, [((w + shift) % CHIPS, w) for w in range(CHIPS)])  20.6 us
    all_to_all x1, blocking collectives, on_device(): cross = lax.all_to_all(cross, ROW, 0, 0, tiled=True)  20.3 us
    ppermute x8, starting transfers between devices, by_chip(): lax.ppermute(x, CHIP, [((w + shift) % CHIPS, w) for w in range(CHIPS)])  18.9 us
    all_to_all x1, blocking collectives, on_device(): spectral = lax.all_to_all(spectral, ROW, 0, 0, tiled=True)  17.1 us
    all_to_all x1, blocking collectives, on_device(): own = lax.all_to_all(block, 'c', 0, 0, tiled=True)  6.77 us
    all_to_all x1, blocking collectives, on_device(): total = lax.all_to_all(total.astype(BF), 'c', 0, 0, tiled=True)  4.08 us
    pallas_call x1, Pallas kernels, on_device(): pl.pallas_call(sums_body, in_specs=[vmem] * 5, out_specs=[vmem] * 5, out_...  2.81 us
  transfers between devices with their start and end apart: 8, of which 5 were waited for; matrix products, arithmetic and copies ran while one was open for 0% of the time, Pallas kernels for 1%

profile of v4, /device:TPU:1, one launch (start us, length us, event | category | flops | bytes accessed | tf_op | source)
XLA Modules:
  0.0 99.4 jit_solution(9966214475434017955)
XLA Ops:
  0.0 1.1 %copy.11 = bf16[128,3,2,128]{0,3,2,1:T(8,128)(2,1)S(1)} copy(bf16[128,3,2,128]{3,2,1,0:T(2,128)(2,1)} %param.7) | data formatting | bytes 393216 | tf_op args[0]
  1.1 0.1 pad_add_fusion.2.at_ref
  1.2 0.7 pad_add_fusion.tables_ref
  1.9 0.8 block.1
  2.7 6.8 %all_to_all.20.g0 = bf16[2,432,128]{2,1,0:T(8,128)(2,1)S(1)} all-to-all(bf16[2,432,128]{2,1,0:T(8,128)(2,1)S(1)} %block.1), channel_id=1, replica_groups=mesh['yh'=2,'z'=8,'c'=2,'yl'=2,'x'=4] {'c'}, dimensions={0} | all-to-all | bytes 442368 | tf_op jit(solution)/shard_map/all_to_all | solution.py:311
  9.5 0.1 fusion
  9.5 2.7 %collective-permute-start.1 = (bf16[2,400,128]{2,1,0:T(8,128)(2,1)S(1)}, bf16[2,400,128]{2,1,0:T(8,128)(2,1)S(1)}, u32[]{:S(2)}, u32[]{:S(2)}) collective-permute-start(bf16[2,400,128]{2,1,0:T(8,128)(2,1)S(1)} %get-tuple-element.28), channel_id=1, source_target_pairs={{208,0},{224,16},{240,32},{0,48},{16,64},{32,80},{48,96},{64,112},... | collective-permute-start | bytes 614408 | tf_op jit(solution)/shard_map/ppermute | solution.py:287
  12.2 4.0 %collective-permute-start = (bf16[2,400,128]{2,1,0:T(8,128)(2,1)S(1)}, bf16[2,400,128]{2,1,0:T(8,128)(2,1)S(1)}, u32[]{:S(2)}, u32[]{:S(2)}) collective-permute-start(bf16[2,400,128]{2,1,0:T(8,128)(2,1)S(1)} %get-tuple-element.28), channel_id=1, source_target_pairs={{16,0},{32,16},{48,32},{64,48},{80,64},{96,80},{112,96},{128,112},... | collective-permute-start | bytes 614408 | tf_op jit(solution)/shard_map/ppermute | solution.py:287
  16.2 2.4 %collective-permute-start.3 = (bf16[2,400,128]{2,1,0:T(8,128)(2,1)S(1)}, bf16[2,400,128]{2,1,0:T(8,128)(2,1)S(1)}, u32[]{:S(2)}, u32[]{:S(2)}) collective-permute-start(bf16[2,400,128]{2,1,0:T(8,128)(2,1)S(1)} %get-tuple-element.27), channel_id=1, source_target_pairs={{128,0},{144,16},{160,32},{176,48},{192,64},{208,80},{224,96},{240... | collective-permute-start | bytes 614408 | tf_op jit(solution)/shard_map/ppermute | solution.py:287
  18.6 0.0 collective-permute-start.2
  18.6 8.6 %collective-permute-done.1.g4 = bf16[2,400,128]{2,1,0:T(8,128)(2,1)S(1)} collective-permute-done((bf16[2,400,128]{2,1,0:T(8,128)(2,1)S(1)}, bf16[2,400,128]{2,1,0:T(8,128)(2,1)S(1)}, u32[]{:S(2)}, u32[]{:S(2)}) %collective-permute-start.1) | collective-permute-done | bytes 204832 | tf_op jit(solution)/shard_map/ppermute | solution.py:287
  27.2 0.0 collective-permute-done.g1
  27.2 0.0 copy-start.2
  27.2 1.3 %early_cross.1 = (bf16[16,208,128]{2,1,0:T(8,128)(2,1)S(1)}, s32[24,128]{1,0:T(8,128)S(1)}, bf16[4,2,384,384]{3,2,1,0:T(8,128)(2,1)S(1)}) custom-call(bf16[2,432,128]{2,1,0:T(8,128)(2,1)S(1)} %all_to_all.20.g0, bf16[2,400,128]{2,1,0:T(8,128)(2,1)S(1)} %collective-permute-done.g1, bf16[2,400,128]{2,1,0:T(8,128)(2,1)S(1)} %collective-permute-done.1.g4), custom_call_target="tpu_custom_call" | custom-call | flops 600000000 | bytes 6291456 | tf_op jit(solution)/shard_map/early_cross/pallas_call | solution.py:318
  28.5 0.0 copy-start
  28.5 0.0 copy-start.1
  28.5 0.0 collective-permute-done.3.g3
  28.5 1.5 %collective-permute-done.2.g2 = bf16[2,400,128]{2,1,0:T(8,128)(2,1)S(1)} collective-permute-done((bf16[2,400,128]{2,1,0:T(8,128)(2,1)S(1)}, bf16[2,400,128]{2,1,0:T(8,128)(2,1)S(1)}, u32[]{:S(2)}, u32[]{:S(2)}) %collective-permute-start.2) | collective-permute-done | bytes 204832 | tf_op jit(solution)/shard_map/ppermute | solution.py:287
  30.0 1.7 %late_cross.1 = (bf16[16,208,128]{2,1,0:T(8,128)(2,1)S(1)}, s32[32,128]{1,0:T(8,128)S(1)}, bf16[5,2,384,384]{3,2,1,0:T(8,128)(2,1)S(1)}) custom-call(bf16[2,432,128]{2,1,0:T(8,128)(2,1)S(1)} %all_to_all.20.g0, bf16[2,400,128]{2,1,0:T(8,128)(2,1)S(1)} %collective-permute-done.g1, ...), custom_call_target="tpu_custom_call", output_to_operand_aliasing={{0}: (5, {})} | custom-call | flops 800000000 | bytes 6291456 | tf_op jit(solution)/shard_map/late_cross/pallas_call | solution.py:327
  31.7 20.3 %all_to_all.21.cross_ref = bf16[16,208,128]{2,1,0:T(8,128)(2,1)S(1)} all-to-all(bf16[16,208,128]{2,1,0:T(8,128)(2,1)S(1)} %get-tuple-element.21), channel_id=1, replica_groups=mesh['yh'=2,'z'=8,'c'=2,'yl'=2,'x'=4] {'c','yl','x'}, dimensions={0} | all-to-all | bytes 1703936 | tf_op jit(solution)/shard_map/all_to_all | solution.py:337
  52.0 0.0 copy-done.2
  52.0 0.0 copy-done
  52.0 0.0 copy-done.1
  52.0 2.0 %spectral.1 = bf16[16,208,128]{2,1,0:T(8,128)(2,1)S(1)} custom-call(bf16[16,208,128]{2,1,0:T(8,128)(2,1)S(1)} %all_to_all.21.cross_ref, bf16[1024,1024]{1,0:T(8,128)(2,1)S(1)} %copy-done.1, bf16[1024,1024]{1,0:T(8,128)(2,1)S(1)} %copy-done, f32[1024,2]{1,0:T(8,128)S(1)} %copy-done.2), custom_call_target="tpu_custom_call" | custom-call | flops 1100000000 | bytes 6291456 | tf_op jit(solution)/shard_map/spectral/pallas_call | solution.py:340
  54.0 17.1 %all_to_all.22.spec_ref = bf16[16,208,128]{2,1,0:T(8,128)(2,1)S(1)} all-to-all(bf16[16,208,128]{2,1,0:T(8,128)(2,1)S(1)} %spectral.1), channel_id=1, replica_groups=mesh['yh'=2,'z'=8,'c'=2,'yl'=2,'x'=4] {'c','yl','x'}, dimensions={0} | all-to-all | bytes 1703936 | tf_op jit(solution)/shard_map/all_to_all | solution.py:354
  71.1 2.8 %sums.1 = (f32[2,384,128]{2,1,0:T(8,128)S(1)}, bf16[2,384,128]{2,1,0:T(8,128)(2,1)S(1)}, bf16[2,384,128]{2,1,0:T(8,128)(2,1)S(1)}, bf16[2,384,128]{2,1,0:T(8,128)(2,1)S(1)}, bf16[2,384,128]{2,1,0:T(8,128)(2,1)S(1)}) custom-call(s32[24,128]{1,0:T(8,128)S(1)} %get-tuple-element.16.early_ref, bf16[4,2,384,384]{3,2,1,0:T(8,128)(2,1)S(1)} %get-tuple-element.17.early_rows, ...), custom_call_target="tpu_custom_call" | custom-call | tf_op jit(solution)/shard_map/sums/pallas_call | solution.py:357
  73.9 2.0 %collective-permute-start.4 = (bf16[2,384,128]{2,1,0:T(8,128)(2,1)S(1)}, bf16[2,384,128]{2,1,0:T(8,128)(2,1)S(1)}, u32[]{:S(2)}, u32[]{:S(2)}) collective-permute-start(bf16[2,384,128]{2,1,0:T(8,128)(2,1)S(1)} %get-tuple-element.23), channel_id=1, source_target_pairs={{240,0},{0,16},{16,32},{32,48},{48,64},{64,80},{80,96},{96,112},{1... | collective-permute-start | bytes 589832 | tf_op jit(solution)/shard_map/ppermute | solution.py:287
  76.0 0.5 collective-permute-start.5
  76.5 4.7 %collective-permute-start.6 = (bf16[2,384,128]{2,1,0:T(8,128)(2,1)S(1)}, bf16[2,384,128]{2,1,0:T(8,128)(2,1)S(1)}, u32[]{:S(2)}, u32[]{:S(2)}) collective-permute-start(bf16[2,384,128]{2,1,0:T(8,128)(2,1)S(1)} %get-tuple-element.25), channel_id=1, source_target_pairs={{48,0},{64,16},{80,32},{96,48},{112,64},{128,80},{144,96},{160,112... | collective-permute-start | bytes 589832 | tf_op jit(solution)/shard_map/ppermute | solution.py:287
  81.2 2.6 %collective-permute-start.7 = (bf16[2,384,128]{2,1,0:T(8,128)(2,1)S(1)}, bf16[2,384,128]{2,1,0:T(8,128)(2,1)S(1)}, u32[]{:S(2)}, u32[]{:S(2)}) collective-permute-start(bf16[2,384,128]{2,1,0:T(8,128)(2,1)S(1)} %get-tuple-element.26), channel_id=1, source_target_pairs={{128,0},{144,16},{160,32},{176,48},{192,64},{208,80},{224,96},{240... | collective-permute-start | bytes 589832 | tf_op jit(solution)/shard_map/ppermute | solution.py:287
  83.8 0.1 collective-permute-done.4
  83.9 6.7 %collective-permute-done.5 = bf16[2,384,128]{2,1,0:T(8,128)(2,1)S(1)} collective-permute-done((bf16[2,384,128]{2,1,0:T(8,128)(2,1)S(1)}, bf16[2,384,128]{2,1,0:T(8,128)(2,1)S(1)}, u32[]{:S(2)}, u32[]{:S(2)}) %collective-permute-start.5) | collective-permute-done | bytes 196640 | tf_op jit(solution)/shard_map/ppermute | solution.py:287
  90.7 3.5 %collective-permute-done.6 = bf16[2,384,128]{2,1,0:T(8,128)(2,1)S(1)} collective-permute-done((bf16[2,384,128]{2,1,0:T(8,128)(2,1)S(1)}, bf16[2,384,128]{2,1,0:T(8,128)(2,1)S(1)}, u32[]{:S(2)}, u32[]{:S(2)}) %collective-permute-start.6) | collective-permute-done | bytes 196640 | tf_op jit(solution)/shard_map/ppermute | solution.py:287
  94.2 0.0 collective-permute-done.7
  94.2 0.1 add_convert_fusion
  94.3 4.1 %all_to_all.23 = bf16[2,384,128]{2,1,0:T(8,128)(2,1)S(1)} all-to-all(bf16[2,384,128]{2,1,0:T(8,128)(2,1)S(1)} %add_convert_fusion), channel_id=1, replica_groups=mesh['yh'=2,'z'=8,'c'=2,'yl'=2,'x'=4] {'c'}, dimensions={0} | all-to-all | bytes 393216 | tf_op jit(solution)/shard_map/all_to_all | solution.py:369
  98.5 0.9 copy.13
  (2 shorter events, 0.1 us)
Async XLA Ops:
  9.5 17.7 %collective-permute-start.1 = (bf16[2,400,128]{2,1,0:T(8,128)(2,1)S(1)}, bf16[2,400,128]{2,1,0:T(8,128)(2,1)S(1)}, u32[]{:S(2)}, u32[]{:S(2)}) collective-permute-start(bf16[2,400,128]{2,1,0:T(8,128)(2,1)S(1)} %get-tuple-element.28), channel_id=1, source_target_pairs={{208,0},{224,16},{240,32},{0,48},{16,64},{32,80},{48,96},{64,112},... | collective-permute-start | bytes 614408 | tf_op jit(solution)/shard_map/ppermute | solution.py:287
  12.2 15.0 %collective-permute-start = (bf16[2,400,128]{2,1,0:T(8,128)(2,1)S(1)}, bf16[2,400,128]{2,1,0:T(8,128)(2,1)S(1)}, u32[]{:S(2)}, u32[]{:S(2)}) collective-permute-start(bf16[2,400,128]{2,1,0:T(8,128)(2,1)S(1)} %get-tuple-element.28), channel_id=1, source_target_pairs={{16,0},{32,16},{48,32},{64,48},{80,64},{96,80},{112,96},{128,112},... | collective-permute-start | bytes 614408 | tf_op jit(solution)/shard_map/ppermute | solution.py:287
  16.2 12.3 %collective-permute-start.3 = (bf16[2,400,128]{2,1,0:T(8,128)(2,1)S(1)}, bf16[2,400,128]{2,1,0:T(8,128)(2,1)S(1)}, u32[]{:S(2)}, u32[]{:S(2)}) collective-permute-start(bf16[2,400,128]{2,1,0:T(8,128)(2,1)S(1)} %get-tuple-element.27), channel_id=1, source_target_pairs={{128,0},{144,16},{160,32},{176,48},{192,64},{208,80},{224,96},{240... | collective-permute-start | bytes 614408 | tf_op jit(solution)/shard_map/ppermute | solution.py:287
  18.6 11.5 %collective-permute-start.2 = (bf16[2,400,128]{2,1,0:T(8,128)(2,1)S(1)}, bf16[2,400,128]{2,1,0:T(8,128)(2,1)S(1)}, u32[]{:S(2)}, u32[]{:S(2)}) collective-permute-start(bf16[2,400,128]{2,1,0:T(8,128)(2,1)S(1)} %get-tuple-element.28), channel_id=1, source_target_pairs={{32,0},{48,16},{64,32},{80,48},{96,64},{112,80},{128,96},{144,112}... | collective-permute-start | bytes 614408 | tf_op jit(solution)/shard_map/ppermute | solution.py:287
  27.2 24.8 %copy-start.2 = (f32[1024,2]{1,0:T(8,128)S(1)}, f32[1024,2]{1,0:T(8,128)}, u32[]{:S(2)}) copy-start(f32[1024,2]{1,0:T(8,128)} %constant.29.clone.diag_ref) | copy-start | bytes 24580
  28.5 23.6 %copy-start = (bf16[1024,1024]{1,0:T(8,128)(2,1)S(1)}, bf16[1024,1024]{1,0:T(8,128)(2,1)}, u32[]{:S(2)}) copy-start(bf16[1024,1024]{1,0:T(8,128)(2,1)} %constant.37.couple_t_ref) | copy-start | bytes 6291460
  28.5 23.5 %copy-start.1 = (bf16[1024,1024]{1,0:T(8,128)(2,1)S(1)}, bf16[1024,1024]{1,0:T(8,128)(2,1)}, u32[]{:S(2)}) copy-start(bf16[1024,1024]{1,0:T(8,128)(2,1)} %constant.36.couple_ref) | copy-start | bytes 6291460
  73.9 10.0 %collective-permute-start.4 = (bf16[2,384,128]{2,1,0:T(8,128)(2,1)S(1)}, bf16[2,384,128]{2,1,0:T(8,128)(2,1)S(1)}, u32[]{:S(2)}, u32[]{:S(2)}) collective-permute-start(bf16[2,384,128]{2,1,0:T(8,128)(2,1)S(1)} %get-tuple-element.23), channel_id=1, source_target_pairs={{240,0},{0,16},{16,32},{32,48},{48,64},{64,80},{80,96},{96,112},{1... | collective-permute-start | bytes 589832 | tf_op jit(solution)/shard_map/ppermute | solution.py:287
  76.0 14.7 %collective-permute-start.5 = (bf16[2,384,128]{2,1,0:T(8,128)(2,1)S(1)}, bf16[2,384,128]{2,1,0:T(8,128)(2,1)S(1)}, u32[]{:S(2)}, u32[]{:S(2)}) collective-permute-start(bf16[2,384,128]{2,1,0:T(8,128)(2,1)S(1)} %get-tuple-element.24), channel_id=1, source_target_pairs={{224,0},{240,16},{0,32},{16,48},{32,64},{48,80},{64,96},{80,112},{... | collective-permute-start | bytes 589832 | tf_op jit(solution)/shard_map/ppermute | solution.py:287
  76.5 17.7 %collective-permute-start.6 = (bf16[2,384,128]{2,1,0:T(8,128)(2,1)S(1)}, bf16[2,384,128]{2,1,0:T(8,128)(2,1)S(1)}, u32[]{:S(2)}, u32[]{:S(2)}) collective-permute-start(bf16[2,384,128]{2,1,0:T(8,128)(2,1)S(1)} %get-tuple-element.25), channel_id=1, source_target_pairs={{48,0},{64,16},{80,32},{96,48},{112,64},{128,80},{144,96},{160,112... | collective-permute-start | bytes 589832 | tf_op jit(solution)/shard_map/ppermute | solution.py:287
  81.2 13.0 %collective-permute-start.7 = (bf16[2,384,128]{2,1,0:T(8,128)(2,1)S(1)}, bf16[2,384,128]{2,1,0:T(8,128)(2,1)S(1)}, u32[]{:S(2)}, u32[]{:S(2)}) collective-permute-start(bf16[2,384,128]{2,1,0:T(8,128)(2,1)S(1)} %get-tuple-element.26), channel_id=1, source_target_pairs={{128,0},{144,16},{160,32},{176,48},{192,64},{208,80},{224,96},{240... | collective-permute-start | bytes 589832 | tf_op jit(solution)/shard_map/ppermute | solution.py:287

commit v5 on v4

--- a/solution.py
+++ b/solution.py
@@ -23,8 +23,8 @@
 TAIL = 32
 NONE = 1024
 WIDE = 4 * SLOTS
-EARLY = (0, 1, 3, 4)
-LATE = (2, 5, 6, 7, 8)
+EARLY = (0, 2, 3, 5)
+LATE = (1, 4, 6, 7, 8)
 ALONE = tuple((gap, a) for gap in (2, 3, 4, 5, 6) for a in range(3)) + ((1, 0),)
 SHARED = ((1, 1), (1, 2), (7, 0), (7, 1), (7, 2), (0, 0), (0, 1), (8, 0))
 RESTS = {(8, 1): range(0, 8), (0, 2): range(8, 10), (8, 2): range(10, 12)}
@@ -137,8 +137,8 @@
                 out_ref[peer, 192:208, :] = rest.astype(BF)
 
 
-def early_cross_body(g0, g1, g4, out_ref, index_ref, rows_ref):
-    groups = {0: by_block(g0, 0), 1: by_block(g1, 1), 4: by_block(g4, 4)}
+def early_cross_body(g0, g2, g4, out_ref, index_ref, rows_ref):
+    groups = {0: by_block(g0, 0), 2: by_block(g2, 2), 4: by_block(g4, 4)}
     fill_index(index_ref, groups, EARLY)
     for n, gap in enumerate(EARLY):
         put_pairs(out_ref, gap, *cross_of(groups, index_ref, rows_ref, n, gap))
@@ -146,7 +146,7 @@
         out_ref[peer, 192:208, :] = jnp.zeros((16, 128), BF)
 
 
-def late_cross_body(g0, g1, g2, g3, g4, begun, out_ref, index_ref, rows_ref):
+def late_cross_body(g0, g2, g4, g3, g1, begun, out_ref, index_ref, rows_ref):
     groups = [by_block(g, place) for place, g in enumerate((g0, g1, g2, g3, g4))]
     fill_index(index_ref, groups, LATE)
     for n, gap in enumerate(LATE):
@@ -323,7 +323,7 @@
         compiler_params=params,
         cost_estimate=pl.CostEstimate(flops=600000000, transcendentals=0, bytes_accessed=6291456),
         name="early_cross",
-    )(groups[0], groups[1], groups[4])
+    )(groups[0], groups[2], groups[4])
     cross, late, late_rows = pl.pallas_call(
         late_cross_body,
         in_specs=[vmem] * 6,
@@ -333,7 +333,7 @@
         compiler_params=params,
         cost_estimate=pl.CostEstimate(flops=800000000, transcendentals=0, bytes_accessed=6291456),
         name="late_cross",
-    )(*groups, cross)
+    )(groups[0], groups[2], groups[4], groups[3], groups[1], cross)
     cross = lax.all_to_all(cross, ROW, 0, 0, tiled=True)
 
     couple, real, imag = operator_parts(freq_total)

time: 99.7 us -> 99.1 us (level)
  transfers between devices with their start and end apart: 8 -> 8, of which waited for: 5 -> 6; matrix products, arithmetic and copies ran while one was open for 0% -> 0% of each run, Pallas kernels for 1% -> 1%
where the time goes in v5:
time: 99.1 us; the launch traced here: 98.8 us
  blocking collectives  48.2 us (49%)
  waiting for transfers between devices  20 us (20%)
  starting transfers between devices  18.9 us (19%)
  Pallas kernels  8.48 us (9%)
  local copies, waits for them, and re-layouts  2.11 us (2%)
    ppermute x8, waiting for transfers between devices, by_chip(): lax.ppermute(x, CHIP, [((w + shift) % CHIPS, w) for w in range(CHIPS)])  20 us
    all_to_all x1, blocking collectives, on_device(): cross = lax.all_to_all(cross, ROW, 0, 0, tiled=True)  19.9 us
    ppermute x8, starting transfers between devices, by_chip(): lax.ppermute(x, CHIP, [((w + shift) % CHIPS, w) for w in range(CHIPS)])  18.9 us
    all_to_all x1, blocking collectives, on_device(): spectral = lax.all_to_all(spectral, ROW, 0, 0, tiled=True)  17.1 us
    all_to_all x1, blocking collectives, on_device(): own = lax.all_to_all(block, 'c', 0, 0, tiled=True)  6.77 us
    all_to_all x1, blocking collectives, on_device(): total = lax.all_to_all(total.astype(BF), 'c', 0, 0, tiled=True)  4.49 us
    pallas_call x1, Pallas kernels, on_device(): pl.pallas_call(sums_body, in_specs=[vmem] * 5, out_specs=[vmem] * 5, out_...  2.81 us
  transfers between devices with their start and end apart: 8, of which 6 were waited for; matrix products, arithmetic and copies ran while one was open for 0% of the time, Pallas kernels for 1%

profile of v5, /device:TPU:1, one launch (start us, length us, event | category | flops | bytes accessed | tf_op | source)
XLA Modules:
  0.0 98.8 jit_solution(12907977515781858820)
XLA Ops:
  0.0 1.1 %copy.11 = bf16[128,3,2,128]{0,3,2,1:T(8,128)(2,1)S(1)} copy(bf16[128,3,2,128]{3,2,1,0:T(2,128)(2,1)} %param.7) | data formatting | bytes 393216 | tf_op args[0]
  1.1 0.1 pad_add_fusion.2.at_ref
  1.2 0.7 pad_add_fusion.tables_ref
  1.9 0.8 block.1
  2.7 6.8 %all_to_all.20.g0 = bf16[2,432,128]{2,1,0:T(8,128)(2,1)S(1)} all-to-all(bf16[2,432,128]{2,1,0:T(8,128)(2,1)S(1)} %block.1), channel_id=1, replica_groups=mesh['yh'=2,'z'=8,'c'=2,'yl'=2,'x'=4] {'c'}, dimensions={0} | all-to-all | bytes 442368 | tf_op jit(solution)/shard_map/all_to_all | solution.py:311
  9.5 0.1 fusion
  9.5 2.7 %collective-permute-start.1 = (bf16[2,400,128]{2,1,0:T(8,128)(2,1)S(1)}, bf16[2,400,128]{2,1,0:T(8,128)(2,1)S(1)}, u32[]{:S(2)}, u32[]{:S(2)}) collective-permute-start(bf16[2,400,128]{2,1,0:T(8,128)(2,1)S(1)} %get-tuple-element.28), channel_id=1, source_target_pairs={{208,0},{224,16},{240,32},{0,48},{16,64},{32,80},{48,96},{64,112},... | collective-permute-start | bytes 614408 | tf_op jit(solution)/shard_map/ppermute | solution.py:287
  12.2 4.4 %collective-permute-start = (bf16[2,400,128]{2,1,0:T(8,128)(2,1)S(1)}, bf16[2,400,128]{2,1,0:T(8,128)(2,1)S(1)}, u32[]{:S(2)}, u32[]{:S(2)}) collective-permute-start(bf16[2,400,128]{2,1,0:T(8,128)(2,1)S(1)} %get-tuple-element.28), channel_id=1, source_target_pairs={{32,0},{48,16},{64,32},{80,48},{96,64},{112,80},{128,96},{144,112}... | collective-permute-start | bytes 614408 | tf_op jit(solution)/shard_map/ppermute | solution.py:287
  16.6 1.5 %collective-permute-start.2 = (bf16[2,400,128]{2,1,0:T(8,128)(2,1)S(1)}, bf16[2,400,128]{2,1,0:T(8,128)(2,1)S(1)}, u32[]{:S(2)}, u32[]{:S(2)}) collective-permute-start(bf16[2,400,128]{2,1,0:T(8,128)(2,1)S(1)} %get-tuple-element.27), channel_id=1, source_target_pairs={{128,0},{144,16},{160,32},{176,48},{192,64},{208,80},{224,96},{240... | collective-permute-start | bytes 614408 | tf_op jit(solution)/shard_map/ppermute | solution.py:287
  18.1 0.5 collective-permute-start.3
  18.6 8.6 %collective-permute-done.1.g4 = bf16[2,400,128]{2,1,0:T(8,128)(2,1)S(1)} collective-permute-done((bf16[2,400,128]{2,1,0:T(8,128)(2,1)S(1)}, bf16[2,400,128]{2,1,0:T(8,128)(2,1)S(1)}, u32[]{:S(2)}, u32[]{:S(2)}) %collective-permute-start.1) | collective-permute-done | bytes 204832 | tf_op jit(solution)/shard_map/ppermute | solution.py:287
  27.2 0.0 collective-permute-done.g2
  27.2 0.0 copy-start.2
  27.2 1.2 %early_cross.1 = (bf16[16,208,128]{2,1,0:T(8,128)(2,1)S(1)}, s32[24,128]{1,0:T(8,128)S(1)}, bf16[4,2,384,384]{3,2,1,0:T(8,128)(2,1)S(1)}) custom-call(bf16[2,432,128]{2,1,0:T(8,128)(2,1)S(1)} %all_to_all.20.g0, bf16[2,400,128]{2,1,0:T(8,128)(2,1)S(1)} %collective-permute-done.g2, bf16[2,400,128]{2,1,0:T(8,128)(2,1)S(1)} %collective-permute-done.1.g4), custom_call_target="tpu_custom_call" | custom-call | flops 600000000 | bytes 6291456 | tf_op jit(solution)/shard_map/early_cross/pallas_call | solution.py:318
  28.5 0.0 copy-start
  28.5 0.0 copy-start.1
  28.5 0.0 collective-permute-done.2.g3
  28.5 1.3 %collective-permute-done.3.g1 = bf16[2,400,128]{2,1,0:T(8,128)(2,1)S(1)} collective-permute-done((bf16[2,400,128]{2,1,0:T(8,128)(2,1)S(1)}, bf16[2,400,128]{2,1,0:T(8,128)(2,1)S(1)}, u32[]{:S(2)}, u32[]{:S(2)}) %collective-permute-start.3) | collective-permute-done | bytes 204832 | tf_op jit(solution)/shard_map/ppermute | solution.py:287
  29.8 1.7 %late_cross.1 = (bf16[16,208,128]{2,1,0:T(8,128)(2,1)S(1)}, s32[32,128]{1,0:T(8,128)S(1)}, bf16[5,2,384,384]{3,2,1,0:T(8,128)(2,1)S(1)}) custom-call(bf16[2,432,128]{2,1,0:T(8,128)(2,1)S(1)} %all_to_all.20.g0, bf16[2,400,128]{2,1,0:T(8,128)(2,1)S(1)} %collective-permute-done.g2, ...), custom_call_target="tpu_custom_call", output_to_operand_aliasing={{0}: (5, {})} | custom-call | flops 800000000 | bytes 6291456 | tf_op jit(solution)/shard_map/late_cross/pallas_call | solution.py:327
  31.4 19.9 %all_to_all.21.cross_ref = bf16[16,208,128]{2,1,0:T(8,128)(2,1)S(1)} all-to-all(bf16[16,208,128]{2,1,0:T(8,128)(2,1)S(1)} %get-tuple-element.21), channel_id=1, replica_groups=mesh['yh'=2,'z'=8,'c'=2,'yl'=2,'x'=4] {'c','yl','x'}, dimensions={0} | all-to-all | bytes 1703936 | tf_op jit(solution)/shard_map/all_to_all | solution.py:337
  51.3 0.0 copy-done.2
  51.3 0.0 copy-done
  51.3 0.0 copy-done.1
  51.3 2.0 %spectral.1 = bf16[16,208,128]{2,1,0:T(8,128)(2,1)S(1)} custom-call(bf16[16,208,128]{2,1,0:T(8,128)(2,1)S(1)} %all_to_all.21.cross_ref, bf16[1024,1024]{1,0:T(8,128)(2,1)S(1)} %copy-done.1, bf16[1024,1024]{1,0:T(8,128)(2,1)S(1)} %copy-done, f32[1024,2]{1,0:T(8,128)S(1)} %copy-done.2), custom_call_target="tpu_custom_call" | custom-call | flops 1100000000 | bytes 6291456 | tf_op jit(solution)/shard_map/spectral/pallas_call | solution.py:340
  53.3 17.1 %all_to_all.22.spec_ref = bf16[16,208,128]{2,1,0:T(8,128)(2,1)S(1)} all-to-all(bf16[16,208,128]{2,1,0:T(8,128)(2,1)S(1)} %spectral.1), channel_id=1, replica_groups=mesh['yh'=2,'z'=8,'c'=2,'yl'=2,'x'=4] {'c','yl','x'}, dimensions={0} | all-to-all | bytes 1703936 | tf_op jit(solution)/shard_map/all_to_all | solution.py:354
  70.4 2.8 %sums.1 = (f32[2,384,128]{2,1,0:T(8,128)S(1)}, bf16[2,384,128]{2,1,0:T(8,128)(2,1)S(1)}, bf16[2,384,128]{2,1,0:T(8,128)(2,1)S(1)}, bf16[2,384,128]{2,1,0:T(8,128)(2,1)S(1)}, bf16[2,384,128]{2,1,0:T(8,128)(2,1)S(1)}) custom-call(s32[24,128]{1,0:T(8,128)S(1)} %get-tuple-element.16.early_ref, bf16[4,2,384,384]{3,2,1,0:T(8,128)(2,1)S(1)} %get-tuple-element.17.early_rows, ...), custom_call_target="tpu_custom_call" | custom-call | tf_op jit(solution)/shard_map/sums/pallas_call | solution.py:357
  73.2 2.7 %collective-permute-start.4 = (bf16[2,384,128]{2,1,0:T(8,128)(2,1)S(1)}, bf16[2,384,128]{2,1,0:T(8,128)(2,1)S(1)}, u32[]{:S(2)}, u32[]{:S(2)}) collective-permute-start(bf16[2,384,128]{2,1,0:T(8,128)(2,1)S(1)} %get-tuple-element.23), channel_id=1, source_target_pairs={{240,0},{0,16},{16,32},{32,48},{48,64},{64,80},{80,96},{96,112},{1... | collective-permute-start | bytes 589832 | tf_op jit(solution)/shard_map/ppermute | solution.py:287
  76.0 1.2 %collective-permute-start.5 = (bf16[2,384,128]{2,1,0:T(8,128)(2,1)S(1)}, bf16[2,384,128]{2,1,0:T(8,128)(2,1)S(1)}, u32[]{:S(2)}, u32[]{:S(2)}) collective-permute-start(bf16[2,384,128]{2,1,0:T(8,128)(2,1)S(1)} %get-tuple-element.24), channel_id=1, source_target_pairs={{224,0},{240,16},{0,32},{16,48},{32,64},{48,80},{64,96},{80,112},{... | collective-permute-start | bytes 589832 | tf_op jit(solution)/shard_map/ppermute | solution.py:287
  77.1 4.2 %collective-permute-start.6 = (bf16[2,384,128]{2,1,0:T(8,128)(2,1)S(1)}, bf16[2,384,128]{2,1,0:T(8,128)(2,1)S(1)}, u32[]{:S(2)}, u32[]{:S(2)}) collective-permute-start(bf16[2,384,128]{2,1,0:T(8,128)(2,1)S(1)} %get-tuple-element.25), channel_id=1, source_target_pairs={{48,0},{64,16},{80,32},{96,48},{112,64},{128,80},{144,96},{160,112... | collective-permute-start | bytes 589832 | tf_op jit(solution)/shard_map/ppermute | solution.py:287
  81.3 1.8 %collective-permute-start.7 = (bf16[2,384,128]{2,1,0:T(8,128)(2,1)S(1)}, bf16[2,384,128]{2,1,0:T(8,128)(2,1)S(1)}, u32[]{:S(2)}, u32[]{:S(2)}) collective-permute-start(bf16[2,384,128]{2,1,0:T(8,128)(2,1)S(1)} %get-tuple-element.26), channel_id=1, source_target_pairs={{128,0},{144,16},{160,32},{176,48},{192,64},{208,80},{224,96},{240... | collective-permute-start | bytes 589832 | tf_op jit(solution)/shard_map/ppermute | solution.py:287
  83.1 1.2 %collective-permute-done.4 = bf16[2,384,128]{2,1,0:T(8,128)(2,1)S(1)} collective-permute-done((bf16[2,384,128]{2,1,0:T(8,128)(2,1)S(1)}, bf16[2,384,128]{2,1,0:T(8,128)(2,1)S(1)}, u32[]{:S(2)}, u32[]{:S(2)}) %collective-permute-start.4) | collective-permute-done | bytes 196640 | tf_op jit(solution)/shard_map/ppermute | solution.py:287
  84.3 6.9 %collective-permute-done.5 = bf16[2,384,128]{2,1,0:T(8,128)(2,1)S(1)} collective-permute-done((bf16[2,384,128]{2,1,0:T(8,128)(2,1)S(1)}, bf16[2,384,128]{2,1,0:T(8,128)(2,1)S(1)}, u32[]{:S(2)}, u32[]{:S(2)}) %collective-permute-start.5) | collective-permute-done | bytes 196640 | tf_op jit(solution)/shard_map/ppermute | solution.py:287
  91.2 0.4 collective-permute-done.6
  91.7 1.5 %collective-permute-done.7 = bf16[2,384,128]{2,1,0:T(8,128)(2,1)S(1)} collective-permute-done((bf16[2,384,128]{2,1,0:T(8,128)(2,1)S(1)}, bf16[2,384,128]{2,1,0:T(8,128)(2,1)S(1)}, u32[]{:S(2)}, u32[]{:S(2)}) %collective-permute-start.7) | collective-permute-done | bytes 196640 | tf_op jit(solution)/shard_map/ppermute | solution.py:287
  93.2 0.1 add_convert_fusion
  93.3 4.5 %all_to_all.23 = bf16[2,384,128]{2,1,0:T(8,128)(2,1)S(1)} all-to-all(bf16[2,384,128]{2,1,0:T(8,128)(2,1)S(1)} %add_convert_fusion), channel_id=1, replica_groups=mesh['yh'=2,'z'=8,'c'=2,'yl'=2,'x'=4] {'c'}, dimensions={0} | all-to-all | bytes 393216 | tf_op jit(solution)/shard_map/all_to_all | solution.py:369
  97.9 0.9 copy.13
  (2 shorter events, 0.1 us)
Async XLA Ops:
  9.5 17.7 %collective-permute-start.1 = (bf16[2,400,128]{2,1,0:T(8,128)(2,1)S(1)}, bf16[2,400,128]{2,1,0:T(8,128)(2,1)S(1)}, u32[]{:S(2)}, u32[]{:S(2)}) collective-permute-start(bf16[2,400,128]{2,1,0:T(8,128)(2,1)S(1)} %get-tuple-element.28), channel_id=1, source_target_pairs={{208,0},{224,16},{240,32},{0,48},{16,64},{32,80},{48,96},{64,112},... | collective-permute-start | bytes 614408 | tf_op jit(solution)/shard_map/ppermute | solution.py:287
  12.2 15.0 %collective-permute-start = (bf16[2,400,128]{2,1,0:T(8,128)(2,1)S(1)}, bf16[2,400,128]{2,1,0:T(8,128)(2,1)S(1)}, u32[]{:S(2)}, u32[]{:S(2)}) collective-permute-start(bf16[2,400,128]{2,1,0:T(8,128)(2,1)S(1)} %get-tuple-element.28), channel_id=1, source_target_pairs={{32,0},{48,16},{64,32},{80,48},{96,64},{112,80},{128,96},{144,112}... | collective-permute-start | bytes 614408 | tf_op jit(solution)/shard_map/ppermute | solution.py:287
  16.6 11.9 %collective-permute-start.2 = (bf16[2,400,128]{2,1,0:T(8,128)(2,1)S(1)}, bf16[2,400,128]{2,1,0:T(8,128)(2,1)S(1)}, u32[]{:S(2)}, u32[]{:S(2)}) collective-permute-start(bf16[2,400,128]{2,1,0:T(8,128)(2,1)S(1)} %get-tuple-element.27), channel_id=1, source_target_pairs={{128,0},{144,16},{160,32},{176,48},{192,64},{208,80},{224,96},{240... | collective-permute-start | bytes 614408 | tf_op jit(solution)/shard_map/ppermute | solution.py:287
  18.1 11.6 %collective-permute-start.3 = (bf16[2,400,128]{2,1,0:T(8,128)(2,1)S(1)}, bf16[2,400,128]{2,1,0:T(8,128)(2,1)S(1)}, u32[]{:S(2)}, u32[]{:S(2)}) collective-permute-start(bf16[2,400,128]{2,1,0:T(8,128)(2,1)S(1)} %get-tuple-element.28), channel_id=1, source_target_pairs={{16,0},{32,16},{48,32},{64,48},{80,64},{96,80},{112,96},{128,112},... | collective-permute-start | bytes 614408 | tf_op jit(solution)/shard_map/ppermute | solution.py:287
  27.2 24.1 %copy-start.2 = (f32[1024,2]{1,0:T(8,128)S(1)}, f32[1024,2]{1,0:T(8,128)}, u32[]{:S(2)}) copy-start(f32[1024,2]{1,0:T(8,128)} %constant.29.clone.diag_ref) | copy-start | bytes 24580
  28.5 22.9 %copy-start = (bf16[1024,1024]{1,0:T(8,128)(2,1)S(1)}, bf16[1024,1024]{1,0:T(8,128)(2,1)}, u32[]{:S(2)}) copy-start(bf16[1024,1024]{1,0:T(8,128)(2,1)} %constant.37.couple_t_ref) | copy-start | bytes 6291460
  28.5 22.9 %copy-start.1 = (bf16[1024,1024]{1,0:T(8,128)(2,1)S(1)}, bf16[1024,1024]{1,0:T(8,128)(2,1)}, u32[]{:S(2)}) copy-start(bf16[1024,1024]{1,0:T(8,128)(2,1)} %constant.36.couple_ref) | copy-start | bytes 6291460
  73.2 11.1 %collective-permute-start.4 = (bf16[2,384,128]{2,1,0:T(8,128)(2,1)S(1)}, bf16[2,384,128]{2,1,0:T(8,128)(2,1)S(1)}, u32[]{:S(2)}, u32[]{:S(2)}) collective-permute-start(bf16[2,384,128]{2,1,0:T(8,128)(2,1)S(1)} %get-tuple-element.23), channel_id=1, source_target_pairs={{240,0},{0,16},{16,32},{32,48},{48,64},{64,80},{80,96},{96,112},{1... | collective-permute-start | bytes 589832 | tf_op jit(solution)/shard_map/ppermute | solution.py:287
  76.0 15.3 %collective-permute-start.5 = (bf16[2,384,128]{2,1,0:T(8,128)(2,1)S(1)}, bf16[2,384,128]{2,1,0:T(8,128)(2,1)S(1)}, u32[]{:S(2)}, u32[]{:S(2)}) collective-permute-start(bf16[2,384,128]{2,1,0:T(8,128)(2,1)S(1)} %get-tuple-element.24), channel_id=1, source_target_pairs={{224,0},{240,16},{0,32},{16,48},{32,64},{48,80},{64,96},{80,112},{... | collective-permute-start | bytes 589832 | tf_op jit(solution)/shard_map/ppermute | solution.py:287
  77.1 14.5 %collective-permute-start.6 = (bf16[2,384,128]{2,1,0:T(8,128)(2,1)S(1)}, bf16[2,384,128]{2,1,0:T(8,128)(2,1)S(1)}, u32[]{:S(2)}, u32[]{:S(2)}) collective-permute-start(bf16[2,384,128]{2,1,0:T(8,128)(2,1)S(1)} %get-tuple-element.25), channel_id=1, source_target_pairs={{48,0},{64,16},{80,32},{96,48},{112,64},{128,80},{144,96},{160,112... | collective-permute-start | bytes 589832 | tf_op jit(solution)/shard_map/ppermute | solution.py:287
  81.3 11.9 %collective-permute-start.7 = (bf16[2,384,128]{2,1,0:T(8,128)(2,1)S(1)}, bf16[2,384,128]{2,1,0:T(8,128)(2,1)S(1)}, u32[]{:S(2)}, u32[]{:S(2)}) collective-permute-start(bf16[2,384,128]{2,1,0:T(8,128)(2,1)S(1)} %get-tuple-element.26), channel_id=1, source_target_pairs={{128,0},{144,16},{160,32},{176,48},{192,64},{208,80},{224,96},{240... | collective-permute-start | bytes 589832 | tf_op jit(solution)/shard_map/ppermute | solution.py:287
